TPU v7x, 32 devices: a whole 2x2x4 slice. The times are simulated.
32 devices in a mesh: seq: 16 (over z, x, core), head: 2 (over y).
Axes of the slice: x: 2, y: 2, z: 4, core: 2. Of those that a mesh axis runs over, the one named last changes fastest.
Arguments:
- channels_in: bfloat16 [2, 12288, 2560], P(None, 'seq', 'head'), may hold values from -6 to 6
- gate_in: bfloat16 [2, 12288, 2560], P(None, 'seq', 'head'), may hold values from -30 to 30
- projections: bfloat16 [2, 2, 12288, 128], P(None, None, 'seq'), may hold values from -1.796875 to 1.796875
- step_raw: bfloat16 [2, 40, 12288], P(None, 'head', 'seq'), may hold values from -4 to 4
- decay_log: float32 [40], P('head'), may hold values from -7 to 2
- step_bias: float32 [40], P('head'), may hold values from -7 to -1
- skip_gain: float32 [40], P('head'), may hold values from 0.3 to 1.2
- norm_gain: float32 [2560], P('head'), may hold values from 0.25 to 1.75
- out_weight: bfloat16 [2560, 1280], P('head'), may hold values from -0.15625 to 0.15625
Outputs:
- mixed: bfloat16 [12288, 2560], P('seq', 'head')
All inputs are finite; a program needn't handle non-finite values.
Results may differ from a plain program's by a relative error of at most 0.017.
Values may be sent and summed in bfloat16 or wider, within the bound.
A program may use at most 128 MiB of HBM per device.

v0:
```python
import functools

import jax
import jax.numpy as jnp
from jax import lax
from jax.experimental import pallas as pl
from jax.experimental.pallas import tpu as pltpu
from jax.sharding import PartitionSpec as P

SUB = 128
PAD = 16
EPS = 1e-05
F32 = jnp.float32
BF16 = jnp.bfloat16


def padded(heads):
    return -(-heads // 8) * 8


def cumulate(values, backward):
    lane = lax.broadcasted_iota(jnp.int32, values.shape, 1)
    own = values
    reach = 1
    while reach < SUB:
        values = values + jnp.where(lane >= reach, pltpu.roll(values, reach, axis=1), 0.0)
        reach *= 2
    total = jnp.broadcast_to(values[:, SUB - 1 :], values.shape)
    if isinstance(backward, bool):
        return (total - values + own if backward else values), total
    return jnp.where(backward, total - values + own, values), total


def steps_of(raw, params):
    step = raw + params[:, 1:2]
    step = jnp.maximum(step, 0.0) + jnp.log1p(jnp.exp(-jnp.abs(step)))
    return step, -step * jnp.exp(params[:, 0:1])


def spreader(rows, columns, width):
    row = lax.broadcasted_iota(jnp.int32, (rows, columns), 0) * width
    column = lax.broadcasted_iota(jnp.int32, (rows, columns), 1)
    one = jnp.where((column >= row) & (column < row + width), 1.0, 0.0)
    return jnp.concatenate([one, one], axis=0).astype(BF16)


def spread(by_head, spread_matrix):
    high = by_head.astype(BF16).astype(F32)
    both = jnp.concatenate([high, by_head - high], axis=0).T.astype(BF16)
    return jnp.dot(both, spread_matrix, preferred_element_type=F32)


def totals_kernel(width, x_ref, b_ref, raw_ref, params_ref, out_ref, raw_scr, scaled):
    heads = raw_ref.shape[1]
    tokens, channels = x_ref.shape[1:]
    state = b_ref.shape[-1]
    raw_scr[...] = jnp.zeros_like(raw_scr)
    raw_scr[:heads, :] = raw_ref[0].astype(F32)
    params = params_ref[...]
    matrix = spreader(raw_scr.shape[0], channels, width)
    backward = pl.program_id(0) == 1
    count = tokens // SUB
    pieces = []
    everything = jnp.zeros((raw_scr.shape[0], SUB), F32)
    for k in range(count):
        step, log_decay = steps_of(raw_scr[:, k * SUB : (k + 1) * SUB], params)
        cumulative, total = cumulate(log_decay, backward)
        pieces.append((step, cumulative, total))
        everything = everything + total
    zero = jnp.zeros_like(everything)
    earlier, later = [zero], [zero]
    for k in range(count - 1):
        earlier.append(earlier[-1] + pieces[k][2])
        later.append(later[-1] + pieces[count - 1 - k][2])
    for k in range(count):
        step, cumulative, total = pieces[k]
        rest = jnp.where(backward, earlier[k], later[count - 1 - k])
        tail = jnp.exp(rest + total - cumulative) * step
        rows = slice(k * SUB, (k + 1) * SUB)
        scaled[rows, :] = (x_ref[0, rows, :].astype(F32) * spread(tail, matrix)).astype(BF16)
    summed = lax.dot_general(
        b_ref[0, 0], scaled[...], (((0,), (0,)), ((), ())), preferred_element_type=F32
    )
    out_ref[0, :state, :] = summed.astype(BF16)
    logs = spread(everything, matrix)[:PAD, :]
    high = logs.astype(BF16).astype(F32)
    row = lax.broadcasted_iota(jnp.int32, logs.shape, 0)
    out_ref[0, state:, :] = jnp.where(row == 0, high, logs - high).astype(BF16)


def carry_kernel(fwd_ref, bwd_ref, out_ref):
    j = pl.program_id(0)
    count = pl.num_programs(0)
    me = lax.axis_index("seq")
    state = out_ref.shape[1]

    @pl.when(j == 0)
    def _():
        out_ref[...] = jnp.zeros_like(out_ref)

    def link(d, ref):
        logs = ref[0, 0, state : state + PAD, :].astype(F32)
        decay = jnp.exp(logs[0:1, :] + logs[1:2, :])
        out_ref[d] = out_ref[d] * decay + ref[0, 0, :state, :].astype(F32)

    @pl.when(j < me)
    def _():
        link(0, fwd_ref)

    @pl.when(count - 1 - j > me)
    def _():
        link(1, bwd_ref)


def scan_kernel(
    width, d_ref, x_ref, gate_ref, b_ref, c_ref, raw_ref, params_ref, gain_ref, w_ref, carry_ref,
    part_ref, square_ref, raw_scr, state_scr, summed,
):
    heads = raw_ref.shape[1]
    rows, channels = x_ref.shape[1:]
    d = d_ref[0]
    backward = d == 1
    params = params_ref[...]
    head_rows = raw_scr.shape[0]
    matrix = spreader(head_rows, channels, width)

    @pl.when(pl.program_id(0) == 0)
    def _():
        state_scr[...] = carry_ref[0]

    raw_scr[...] = jnp.zeros_like(raw_scr)
    raw_scr[:heads, :] = raw_ref[0].astype(F32)
    skip = spread(jnp.broadcast_to(params[:, 2:3], (head_rows, SUB)), matrix)[0:1, :]
    t_index = lax.broadcasted_iota(jnp.int32, (SUB, SUB), 0)
    s_index = lax.broadcasted_iota(jnp.int32, (SUB, SUB), 1)
    sign = 1 - 2 * d
    seen = (t_index - s_index) * sign >= 0
    lane = lax.broadcasted_iota(jnp.int32, (SUB, 2 * width), 1)
    low = jnp.where(lane < width, 1.0, 0.0).astype(BF16)
    high = jnp.where(lane >= width, 1.0, 0.0).astype(BF16)
    subs = rows // SUB
    for i in range(subs):
        at = pl.multiple_of((i + d * (subs - 1 - 2 * i)) * SUB, SUB)
        here = pl.ds(at, SUB)
        step, log_decay = steps_of(raw_scr[:, here], params)
        cumulative, total = cumulate(log_decay, backward)
        rowterm = cumulative - jnp.log(step)
        columns = cumulative.T
        entry_decay = spread(jnp.exp(cumulative), matrix)
        tail = spread(jnp.exp(total - cumulative) * step, matrix)
        read = c_ref[0, 0, here, :]
        write = b_ref[0, 0, here, :]
        scores = lax.dot_general(
            read, write, (((1,), (1,)), ((), ())), preferred_element_type=F32
        )
        x = x_ref[0, here, :]
        wide = x.astype(F32)
        carried = jnp.dot(read, state_scr[...].astype(BF16), preferred_element_type=F32)
        summed[here, :] = carried * entry_decay + skip * wide
        for first in range(0, heads, 2):
            weights = []
            for h in range(first, min(first + 2, heads)):
                power = jnp.where(seen, columns[:, h : h + 1] - rowterm[h : h + 1, :], -1e30)
                weights.append((jnp.exp(power) * scores).astype(BF16))
            span = slice(first * width, (first + len(weights)) * width)
            some_x = x[:, span]
            if len(weights) == 2:
                weights = [jnp.concatenate(weights, axis=1)]
                some_x = jnp.concatenate([some_x * low, some_x * high], axis=0)
            summed[here, span] += jnp.dot(weights[0], some_x, preferred_element_type=F32)
        fresh = lax.dot_general(
            write, (wide * tail).astype(BF16), (((0,), (0,)), ((), ())),
            preferred_element_type=F32,
        )
        decay = jnp.where(backward, entry_decay[0:1, :], entry_decay[SUB - 1 :, :])
        state_scr[...] = state_scr[...] * decay + fresh
    scanned = summed[...].astype(BF16).astype(F32)
    gate = gate_ref[0].astype(F32)
    gated = scanned * (gate / (1.0 + jnp.exp(-gate)))
    square_ref[...] = jnp.sum(gated * gated, axis=1, keepdims=True)
    part = jnp.dot(
        (gated * gain_ref[...]).astype(BF16), w_ref[...], preferred_element_type=F32
    ).astype(BF16)

    @pl.when(d == 0)
    def _():
        part_ref[...] = part

    @pl.when(d == 1)
    def _():
        flip = jnp.where(t_index + s_index == SUB - 1, 1.0, 0.0).astype(BF16)
        blocks = part.shape[1] // SUB
        for k in range(blocks):
            taken = part[:, (blocks - 1 - k) * SUB : (blocks - k) * SUB]
            part_ref[:, k * SUB : (k + 1) * SUB] = jnp.dot(
                taken, flip, preferred_element_type=F32
            ).astype(BF16)


def per_device(
    channels_in, gate_in, projections, step_raw, decay_log, step_bias, skip_gain, norm_gain,
    out_weight,
):
    tokens, channels = channels_in.shape[1:]
    heads = step_raw.shape[1]
    width = channels // heads
    state = projections.shape[-1]
    half = out_weight.shape[1]
    groups = lax.axis_size("head")
    inner = groups * channels
    devices = lax.axis_size("seq")
    block = 2 * SUB if tokens % (2 * SUB) == 0 else SUB
    blocks = tokens // block
    head_rows = padded(heads)
    params = jnp.pad(
        jnp.stack([decay_log, step_bias, skip_gain], axis=1), ((0, head_rows - heads), (0, 0))
    )

    totals = pl.pallas_call(
        functools.partial(totals_kernel, width),
        out_shape=jax.ShapeDtypeStruct((2, state + PAD, channels), BF16),
        grid=(2,),
        in_specs=[
            pl.BlockSpec((1, tokens, channels), lambda d: (d, 0, 0)),
            pl.BlockSpec((1, 1, tokens, state), lambda d: (d, 0, 0, 0)),
            pl.BlockSpec((1, heads, tokens), lambda d: (d, 0, 0)),
            pl.BlockSpec((head_rows, 3), lambda d: (0, 0)),
        ],
        out_specs=pl.BlockSpec((1, state + PAD, channels), lambda d: (d, 0, 0)),
        scratch_shapes=[pltpu.VMEM((head_rows, tokens), F32), pltpu.VMEM((tokens, channels), BF16)],
        name="totals",
    )(channels_in, projections, step_raw, params)

    gathered = lax.all_gather(totals, "seq")
    carries = pl.pallas_call(
        carry_kernel,
        out_shape=jax.ShapeDtypeStruct((2, state, channels), F32),
        grid=(devices,),
        in_specs=[
            pl.BlockSpec((1, 1, state + PAD, channels), lambda j: (j, 0, 0, 0)),
            pl.BlockSpec((1, 1, state + PAD, channels), lambda j: (devices - 1 - j, 1, 0, 0)),
        ],
        out_specs=pl.BlockSpec((2, state, channels), lambda j: (0, 0, 0)),
        name="carry",
    )(gathered, gathered)

    def place(k, d):
        return k + d[0] * (blocks - 1 - 2 * k)

    def scan(d):
        return pl.pallas_call(
            functools.partial(scan_kernel, width),
            out_shape=(
                jax.ShapeDtypeStruct((tokens, half), BF16),
                jax.ShapeDtypeStruct((tokens, 1), F32),
            ),
            grid_spec=pltpu.PrefetchScalarGridSpec(
                num_scalar_prefetch=1,
                grid=(blocks,),
                in_specs=[
                    pl.BlockSpec((1, block, channels), lambda k, d: (d[0], place(k, d), 0)),
                    pl.BlockSpec((1, block, channels), lambda k, d: (d[0], place(k, d), 0)),
                    pl.BlockSpec((1, 1, block, state), lambda k, d: (d[0], 0, place(k, d), 0)),
                    pl.BlockSpec((1, 1, block, state), lambda k, d: (d[0], 1, place(k, d), 0)),
                    pl.BlockSpec((1, heads, block), lambda k, d: (d[0], 0, place(k, d))),
                    pl.BlockSpec((head_rows, 3), lambda k, d: (0, 0)),
                    pl.BlockSpec((1, channels), lambda k, d: (0, 0)),
                    pl.BlockSpec((channels, half), lambda k, d: (0, 0)),
                    pl.BlockSpec((1, state, channels), lambda k, d: (d[0], 0, 0)),
                ],
                out_specs=[
                    pl.BlockSpec((block, half), lambda k, d: (place(k, d), 0)),
                    pl.BlockSpec((block, 1), lambda k, d: (place(k, d), 0)),
                ],
                scratch_shapes=[
                    pltpu.VMEM((head_rows, block), F32),
                    pltpu.VMEM((state, channels), F32),
                    pltpu.VMEM((block, channels), F32),
                ],
            ),
            cost_estimate=pl.CostEstimate(
                flops=4 * tokens * channels * half,
                bytes_accessed=6 * tokens * channels + 2 * channels * half,
                transcendentals=0,
            ),
            name="scan",
        )(
            d.astype(jnp.int32).reshape(1), channels_in, gate_in, projections, projections,
            step_raw, params, norm_gain[None], out_weight, carries,
        )

    group = lax.axis_index("head")
    if groups == 2:
        swap = [(0, 1), (1, 0)]
        part, square = scan(1 - group)
        part = lax.ppermute(part, "head", swap)
        square = lax.ppermute(square, "head", swap)
        own_part, own_square = scan(group)
        summed = own_part.astype(F32) + part.astype(F32)
        squares = own_square + square
    else:
        results = [scan(jnp.asarray(d)) for d in range(2)]
        summed = lax.psum_scatter(
            jnp.concatenate([results[0][0], results[1][0]], axis=1),
            "head", scatter_dimension=1, tiled=True,
        ).astype(F32)
        both = lax.psum(jnp.stack([results[0][1], results[1][1]]), "head")
        squares = jnp.where(2 * group >= groups, both[1], both[0])
    return (summed * lax.rsqrt(squares / inner + EPS)).astype(BF16)


def solution(mesh):
    placed = (
        P(None, "seq", "head"),
        P(None, "seq", "head"),
        P(None, None, "seq", None),
        P(None, "head", "seq"),
        P("head"),
        P("head"),
        P("head"),
        P("head"),
        P("head", None),
    )
    return jax.shard_map(
        per_device, mesh=mesh, in_specs=placed, out_specs=P("seq", "head"), check_vma=False
    )
```

profile of v0, /device:TPU:0, one launch (start us, length us, event | category | flops | bytes accessed | tf_op | source)
XLA Modules:
  0.0 209.0 jit_solution(2299610715127632519)
XLA Ops:
  6.5 0.0 copy-start
  6.5 0.0 all-gather.3.cloned.1.call-start
  6.5 1.5 copy.24.raw_ref
  8.0 0.7 pad_maximum_fusion
  8.7 0.1 copy.22
  8.8 0.6 pad.4.params_ref
  9.4 6.0 %totals.1 = bf16[2,144,1280]{2,1,0:T(8,128)(2,1)} custom-call(bf16[2,768,1280]{2,1,0:T(8,128)(2,1)} %x_ref.5, bf16[2,2,768,128]{3,2,1,0:T(8,128)(2,1)} %c_ref.3, bf16[2,20,768]{2,1,0:T(8,128)(2,1)} %copy.24.raw_ref, f32[24,3]{1,0:T(8,128)} %pad.4.params_ref), custom_call_target="tpu_custom_call" | custom-call | tf_op jit(solution)/shard_map/totals/pallas_call | solution.py:219
  15.4 0.0 all-gather.3.cloned.1.call-update
  15.4 0.0 copy-done
  15.4 0.6 broadcast_in_dim.4.gain_ref
  16.0 97.9 %all-gather.3.cloned.1.call-done = bf16[32,144,1280]{2,1,0:T(8,128)(2,1)} async-done(((bf16[2,144,1280]{2,1,0:T(8,128)(2,1)}), bf16[32,144,1280]{2,1,0:T(8,128)(2,1)}) %all-gather.3.cloned.1.call-update) | async-done | bytes 11796496 | tf_op jit(solution)/shard_map/all_gather | solution.py:234
  113.9 11.2 %carry.1.carry_ref = f32[2,128,1280]{2,1,0:T(8,128)} custom-call(bf16[16,2,144,1280]{3,2,1,0:T(8,128)(2,1)} %bitcast.6, bf16[16,2,144,1280]{3,2,1,0:T(8,128)(2,1)} %bitcast.7), custom_call_target="tpu_custom_call" | custom-call | tf_op jit(solution)/shard_map/carry/pallas_call | solution.py:235
  125.0 18.9 %scan.3 = (bf16[768,1280]{1,0:T(8,128)(2,1)}, f32[768,1]{1,0:T(8,128)}) custom-call(s32[1]{0:T(128)} %bitcast.5.d_ref, bf16[2,768,1280]{2,1,0:T(8,128)(2,1)} %x_ref.5, bf16[2,768,1280]{2,1,0:T(8,128)(2,1)} %gate_ref.3, bf16[2,2,768,128]{3,2,1,0:T(8,128)(2,1)} %c_ref.3, bf16[2,2,768,128]{3,2,1,0:T(8,128)(2,1)} %c_ref.3, bf16[2,20,768]{2,1,0:T(8,128)(2,1)} %copy.24.raw_ref, ...), custom_call_target="tpu_custom_call" | custom-call | flops 5033164800 | bytes 9175040 | tf_op jit(solution)/shard_map/scan/pallas_call | solution.py:251
  143.9 0.7 collective-permute-start
  144.6 1.4 collective-permute-start.1
  145.9 18.1 %scan.2 = (bf16[768,1280]{1,0:T(8,128)(2,1)}, f32[768,1]{1,0:T(8,128)}) custom-call(s32[1]{0:T(128)} %bitcast.d_ref, bf16[2,768,1280]{2,1,0:T(8,128)(2,1)} %x_ref.5, bf16[2,768,1280]{2,1,0:T(8,128)(2,1)} %gate_ref.3, bf16[2,2,768,128]{3,2,1,0:T(8,128)(2,1)} %c_ref.3, bf16[2,2,768,128]{3,2,1,0:T(8,128)(2,1)} %c_ref.3, bf16[2,20,768]{2,1,0:T(8,128)(2,1)} %copy.24.raw_ref, ...), custom_call_target="tpu_custom_call" | custom-call | flops 5033164800 | bytes 9175040 | tf_op jit(solution)/shard_map/scan/pallas_call | solution.py:251
  164.0 33.5 %collective-permute-done.1 = f32[768,1]{1,0:T(8,128)S(1)} collective-permute-done((f32[768,1]{1,0:T(8,128)}, f32[768,1]{1,0:T(8,128)S(1)}, u32[]{:S(2)}, u32[]{:S(2)}) %collective-permute-start.1) | collective-permute-done | bytes 3104 | tf_op jit(solution)/shard_map/ppermute | solution.py:297
  197.6 1.2 rsqrt_reduce_fusion
  198.7 0.0 collective-permute-done
  198.7 3.4 %multiply_convert_fusion = bf16[768,1280]{1,0:T(8,128)(2,1)} fusion(bf16[768,1280]{1,0:T(8,128)(2,1)S(1)} %collective-permute-done, bf16[768,1280]{1,0:T(8,128)(2,1)} %get-tuple-element.9, f32[768]{0:T(1024)S(1)} %rsqrt_reduce_fusion), kind=kLoop, calls=%fused_computation | loop fusion | flops 4915200 | bytes 5901312 | tf_op jit(solution)/shard_map/convert_element_type | solution.py:309
Async XLA Ops:
  6.5 8.9 %copy-start = (f32[1280]{0:T(1024)S(1)}, f32[1280]{0:T(1024)}, u32[]{:S(2)}) copy-start(f32[1280]{0:T(1024)} %param.16) | copy-start | bytes 15364
  6.5 107.3 %all-gather.3.cloned.1.call-start = ((), (), s32[]{:S(2)}) async-start(), calls=%async_computation | async-start | bytes 12533760 | tf_op jit(solution)/shard_map/all_gather | solution.py:234
  143.9 54.9 %collective-permute-start = (bf16[768,1280]{1,0:T(8,128)(2,1)}, bf16[768,1280]{1,0:T(8,128)(2,1)S(1)}, u32[]{:S(2)}, u32[]{:S(2)}) collective-permute-start(bf16[768,1280]{1,0:T(8,128)(2,1)} %get-tuple-element.10), channel_id=1, source_target_pairs={{0,1},{1,0},{2,3},{3,2},{4,5},{5,4},{6,7},{7,6},{8,9},{9,8},{10,11... | collective-permute-start | bytes 5898248 | tf_op jit(solution)/shard_map/ppermute | solution.py:296
  144.6 53.0 %collective-permute-start.1 = (f32[768,1]{1,0:T(8,128)}, f32[768,1]{1,0:T(8,128)S(1)}, u32[]{:S(2)}, u32[]{:S(2)}) collective-permute-start(f32[768,1]{1,0:T(8,128)} %get-tuple-element.12), channel_id=1, source_target_pairs={{0,1},{1,0},{2,3},{3,2},{4,5},{5,4},{6,7},{7,6},{8,9},{9,8},{10,11... | collective-permute-start | bytes 9224 | tf_op jit(solution)/shard_map/ppermute | solution.py:297
Sparse Core Ops, SparseCore 0:
  15.5 98.3 all-gather.2
where the time goes:
time: 209 us
  waiting for transfers between devices  131 us (63%)
  Pallas kernels  54.1 us (26%)
  between operations  13.4 us (6%)
  other arithmetic  5.29 us (3%)
  local copies, waits for them, and re-layouts  2.77 us (1%)
    all_gather x1, waiting for transfers between devices, per_device(): gathered = lax.all_gather(totals, 'seq')  97.9 us
    pallas_call x2, Pallas kernels, scan(): pl.pallas_call(functools.partial(scan_kernel, width), out_shape=(jax.Shap...  37 us
    ppermute x1, waiting for transfers between devices, per_device(): square = lax.ppermute(square, 'head', swap)  33.5 us
    pallas_call x1, Pallas kernels, per_device(): pl.pallas_call(carry_kernel, out_shape=jax.ShapeDtypeStruct((2, state, ch...  11.2 us
    pallas_call x1, Pallas kernels, per_device(): pl.pallas_call(functools.partial(totals_kernel, width), out_shape=jax.Sha...  5.95 us
  transfers between devices with their start and end apart: 3, of which 2 were waited for; matrix products, arithmetic and copies ran while one was open for 1% of the time, Pallas kernels for 9%

commit v1 on v0

--- a/solution.py
+++ b/solution.py
@@ -1,4 +1,5 @@
 import functools
+import math
 
 import jax
 import jax.numpy as jnp
@@ -50,7 +51,9 @@
     return jnp.dot(both, spread_matrix, preferred_element_type=F32)
 
 
-def totals_kernel(width, x_ref, b_ref, raw_ref, params_ref, out_ref, raw_scr, scaled):
+def totals_kernel(
+    width, x_ref, b_ref, raw_ref, params_ref, out_ref, log_ref, raw_scr, scaled
+):
     heads = raw_ref.shape[1]
     tokens, channels = x_ref.shape[1:]
     state = b_ref.shape[-1]
@@ -81,35 +84,130 @@
     summed = lax.dot_general(
         b_ref[0, 0], scaled[...], (((0,), (0,)), ((), ())), preferred_element_type=F32
     )
-    out_ref[0, :state, :] = summed.astype(BF16)
-    logs = spread(everything, matrix)[:PAD, :]
-    high = logs.astype(BF16).astype(F32)
-    row = lax.broadcasted_iota(jnp.int32, logs.shape, 0)
-    out_ref[0, state:, :] = jnp.where(row == 0, high, logs - high).astype(BF16)
-
-
-def carry_kernel(fwd_ref, bwd_ref, out_ref):
-    j = pl.program_id(0)
-    count = pl.num_programs(0)
-    me = lax.axis_index("seq")
-    state = out_ref.shape[1]
-
-    @pl.when(j == 0)
-    def _():
-        out_ref[...] = jnp.zeros_like(out_ref)
-
-    def link(d, ref):
-        logs = ref[0, 0, state : state + PAD, :].astype(F32)
-        decay = jnp.exp(logs[0:1, :] + logs[1:2, :])
-        out_ref[d] = out_ref[d] * decay + ref[0, 0, :state, :].astype(F32)
-
-    @pl.when(j < me)
-    def _():
-        link(0, fwd_ref)
-
-    @pl.when(count - 1 - j > me)
-    def _():
-        link(1, bwd_ref)
+    out_ref[0] = summed.astype(BF16)
+    rest = jnp.zeros((SUB - everything.shape[0], SUB), F32)
+    log_ref[0] = packed_row(jnp.concatenate([everything, rest], axis=0).T[0:1, :])
+
+
+def packed_row(row):
+    row = jnp.broadcast_to(row, (PAD, row.shape[1]))
+    high = row.astype(BF16).astype(F32)
+    index = lax.broadcasted_iota(jnp.int32, row.shape, 0)
+    return jnp.where(index == 0, high, jnp.where(index == 1, row - high, 0.0)).astype(BF16)
+
+
+def carry_kernel(
+    width, mates, planes, state_ref, log_ref, out_ref, one_state, one_log, sum_state, sum_log,
+    two_state, two_log, entry, mine, three_state, send_sem, recv_sem,
+):
+    device = lax.axis_index("seq")
+    plane, spot = device // mates, device % mates
+    rows = one_state.shape[2]
+    channels = state_ref.shape[-1]
+    matrix = spreader(SUB, channels, width)[:SUB]
+
+    def remote(source, target, which, slot, device_id):
+        return pltpu.make_async_remote_copy(
+            src_ref=source, dst_ref=target, send_sem=send_sem.at[which],
+            recv_sem=recv_sem.at[slot], device_id={"seq": device_id},
+            device_id_type=pl.DeviceIdType.MESH,
+        )
+
+    def rows_of(q):
+        return pl.ds(pl.multiple_of(q * rows, rows), rows)
+
+    def decay_of(packed):
+        both = jnp.dot(packed, matrix, preferred_element_type=F32)
+        return jnp.exp(both[0:1, :] + both[1:2, :])
+
+    others = [(spot + o) % mates for o in range(1, mates)]
+    far = [(plane + o) % planes for o in range(1, planes)]
+    barrier = pltpu.get_barrier_semaphore()
+    for q in others:
+        pl.semaphore_signal(
+            barrier, inc=1, device_id={"seq": plane * mates + q},
+            device_id_type=pl.DeviceIdType.MESH,
+        )
+    for p in far:
+        pl.semaphore_signal(
+            barrier, inc=1, device_id={"seq": p * mates + spot},
+            device_id_type=pl.DeviceIdType.MESH,
+        )
+    pl.semaphore_wait(barrier, mates + planes - 2)
+
+    base = 0
+    started = []
+    for o, q in enumerate(others):
+        to = plane * mates + q
+        started.append(
+            remote(state_ref.at[:, rows_of(q)], one_state.at[spot], base + 2 * o, base + 2 * spot, to)
+        )
+        started.append(
+            remote(log_ref, one_log.at[spot], base + 2 * o + 1, base + 2 * spot + 1, to)
+        )
+    for copy in started:
+        copy.start()
+    one_state[spot] = state_ref[:, rows_of(spot), :]
+    one_log[spot] = log_ref[...]
+    for o, q in enumerate(others):
+        remote(one_state.at[q], one_state.at[q], base + 2 * o, base + 2 * q, device).wait_recv()
+        remote(one_log.at[q], one_log.at[q], base + 2 * o + 1, base + 2 * q + 1, device).wait_recv()
+
+    decays = [[decay_of(one_log[q, d]) for q in range(mates)] for d in range(2)]
+    orders = [list(range(mates)), list(range(mates))[::-1]]
+    for d in range(2):
+        total = None
+        logs = None
+        for q in orders[d]:
+            part = one_state[q, d].astype(F32)
+            log = one_log[q, d].astype(F32)
+            total = part if total is None else total * decays[d][q] + part
+            logs = log if logs is None else logs + log
+        sum_state[d] = total.astype(BF16)
+        sum_log[d] = packed_row(logs[0:1, :] + logs[1:2, :])
+    base = 2 * mates
+    for o, p in enumerate(far):
+        d = jnp.where(p > plane, 0, 1)
+        to = p * mates + spot
+        for j, (source, target) in enumerate(((sum_state, two_state), (sum_log, two_log))):
+            copy = remote(
+                source.at[d], target.at[plane], base + 2 * o + j, base + 2 * plane + j, to
+            )
+            copy.start()
+            started.append(copy)
+    for o, p in enumerate(far):
+        for j, target in enumerate((two_state, two_log)):
+            remote(
+                target.at[p], target.at[p], base + 2 * o + j, base + 2 * p + j, device
+            ).wait_recv()
+    entry[...] = jnp.zeros_like(entry)
+
+    def link(d, p):
+        entry[d] = entry[d] * decay_of(two_log[p]) + two_state[p].astype(F32)
+
+    for p in range(planes):
+        pl.when(p < plane)(functools.partial(link, 0, p))
+        pl.when(planes - 1 - p > plane)(functools.partial(link, 1, planes - 1 - p))
+
+    base = 2 * mates + 2 * planes
+    for d in range(2):
+        carried = entry[d]
+        for q in orders[d]:
+            mine[q, d] = carried.astype(BF16)
+            if q != orders[d][-1]:
+                carried = carried * decays[d][q] + one_state[q, d].astype(F32)
+    for o, q in enumerate(others):
+        copy = remote(mine.at[q], three_state.at[spot], base + o, base + spot, plane * mates + q)
+        copy.start()
+        started.append(copy)
+    three_state[spot] = mine[spot]
+    for o, q in enumerate(others):
+        remote(three_state.at[q], three_state.at[q], base + o, base + q, device).wait_recv()
+    for q in range(mates):
+        for d in range(2):
+            out_ref[d, q * rows : (q + 1) * rows, :] = three_state[q, d].astype(F32)
+    for copy in started:
+        copy.wait_send()
 
 
 def scan_kernel(
@@ -216,9 +314,12 @@
         jnp.stack([decay_log, step_bias, skip_gain], axis=1), ((0, head_rows - heads), (0, 0))
     )
 
-    totals = pl.pallas_call(
+    totals, logs = pl.pallas_call(
         functools.partial(totals_kernel, width),
-        out_shape=jax.ShapeDtypeStruct((2, state + PAD, channels), BF16),
+        out_shape=(
+            jax.ShapeDtypeStruct((2, state, channels), BF16),
+            jax.ShapeDtypeStruct((2, PAD, SUB), BF16),
+        ),
         grid=(2,),
         in_specs=[
             pl.BlockSpec((1, tokens, channels), lambda d: (d, 0, 0)),
@@ -226,23 +327,39 @@
             pl.BlockSpec((1, heads, tokens), lambda d: (d, 0, 0)),
             pl.BlockSpec((head_rows, 3), lambda d: (0, 0)),
         ],
-        out_specs=pl.BlockSpec((1, state + PAD, channels), lambda d: (d, 0, 0)),
+        out_specs=[
+            pl.BlockSpec((1, state, channels), lambda d: (d, 0, 0)),
+            pl.BlockSpec((1, PAD, SUB), lambda d: (d, 0, 0)),
+        ],
         scratch_shapes=[pltpu.VMEM((head_rows, tokens), F32), pltpu.VMEM((tokens, channels), BF16)],
         name="totals",
     )(channels_in, projections, step_raw, params)
 
-    gathered = lax.all_gather(totals, "seq")
+    mates = math.gcd(devices, 4)
+    planes = devices // mates
+    share = state // mates
+    copies = 3 * mates + 2 * planes
     carries = pl.pallas_call(
-        carry_kernel,
+        functools.partial(carry_kernel, width, mates, planes),
         out_shape=jax.ShapeDtypeStruct((2, state, channels), F32),
-        grid=(devices,),
-        in_specs=[
-            pl.BlockSpec((1, 1, state + PAD, channels), lambda j: (j, 0, 0, 0)),
-            pl.BlockSpec((1, 1, state + PAD, channels), lambda j: (devices - 1 - j, 1, 0, 0)),
+        in_specs=[pl.BlockSpec(memory_space=pltpu.VMEM)] * 2,
+        out_specs=pl.BlockSpec(memory_space=pltpu.VMEM),
+        scratch_shapes=[
+            pltpu.VMEM((mates, 2, share, channels), BF16),
+            pltpu.VMEM((mates, 2, PAD, SUB), BF16),
+            pltpu.VMEM((2, share, channels), BF16),
+            pltpu.VMEM((2, PAD, SUB), BF16),
+            pltpu.VMEM((planes, share, channels), BF16),
+            pltpu.VMEM((planes, PAD, SUB), BF16),
+            pltpu.VMEM((2, share, channels), F32),
+            pltpu.VMEM((mates, 2, share, channels), BF16),
+            pltpu.VMEM((mates, 2, share, channels), BF16),
+            pltpu.SemaphoreType.DMA((copies,)),
+            pltpu.SemaphoreType.DMA((copies,)),
         ],
-        out_specs=pl.BlockSpec((2, state, channels), lambda j: (0, 0, 0)),
+        compiler_params=pltpu.CompilerParams(collective_id=0, has_side_effects=True),
         name="carry",
-    )(gathered, gathered)
+    )(totals, logs)
 
     def place(k, d):
         return k + d[0] * (blocks - 1 - 2 * k)

time: 209 us -> 119 us (0.57)
  waiting for transfers between devices: 131 us -> 34 us
  Pallas kernels: 54.1 us -> 73.9 us
  between operations: 13.4 us -> 0.02 us
    all_gather x1 -> x0, waiting for transfers between devices: 97.9 us -> none  [per_device(): gathered = lax.all_gather(totals, 'seq')]
    pallas_call x2, Pallas kernels: 17.1 us -> 36.9 us  [the longest x1 31 us: per_device(): pl.pallas_call(functools.partial(carry_kernel, width, mates, planes), out...]
  transfers between devices with their start and end apart: 3 -> 2, of which waited for: 2 -> 1; matrix products, arithmetic and copies ran while one was open for 1% -> 1% of each run, Pallas kernels for 9% -> 15%
where the time goes in v1:
time: 119 us
  Pallas kernels  73.9 us (62%)
  waiting for transfers between devices  34 us (29%)
  other arithmetic  5.29 us (4%)
  local copies, waits for them, and re-layouts  3.46 us (3%)
  starting transfers between devices  2.03 us (2%)
    pallas_call x2, Pallas kernels, scan(): pl.pallas_call(functools.partial(scan_kernel, width), out_shape=(jax.Shap...  37 us
    ppermute x1, waiting for transfers between devices, per_device(): square = lax.ppermute(square, 'head', swap)  34 us
    pallas_call x1, Pallas kernels, per_device(): pl.pallas_call(functools.partial(carry_kernel, width, mates, planes), out...  31 us
    pallas_call x1, Pallas kernels, per_device(): pl.pallas_call(functools.partial(totals_kernel, width), out_shape=(jax.Sh...  5.93 us
    convert_element_type x1, other arithmetic, per_device(): return (summed * lax.rsqrt(squares / inner + EPS)).astype(BF16)  3.41 us
  transfers between devices with their start and end apart: 2, of which 1 were waited for; matrix products, arithmetic and copies ran while one was open for 1% of the time, Pallas kernels for 15%

profile of v1, /device:TPU:0, one launch (start us, length us, event | category | flops | bytes accessed | tf_op | source)
XLA Modules:
  0.0 118.7 jit_solution(12986320445379412933)
XLA Ops:
  0.0 1.3 %broadcast_in_dim.4.gain_ref = f32[1,1280]{1,0:T(1,128)} reshape(f32[1280]{0:T(1024)} %param.16) | data formatting | bytes 10240 | tf_op jit(solution)/shard_map/broadcast_in_dim | solution.py:406
  1.3 0.7 pad_maximum_fusion
  2.0 0.1 copy.22
  2.1 1.5 %copy.24.raw_ref = bf16[2,20,768]{2,1,0:T(8,128)(2,1)} copy(bf16[2,20,768]{2,0,1:T(2,128)(2,1)} %param.12) | data formatting | bytes 122880 | tf_op args[3]
  3.6 0.6 pad.4.params_ref
  4.2 5.9 %totals.1 = (bf16[2,128,1280]{2,1,0:T(8,128)(2,1)}, bf16[2,16,128]{2,1,0:T(8,128)(2,1)}) custom-call(bf16[2,768,1280]{2,1,0:T(8,128)(2,1)} %x_ref.5, bf16[2,2,768,128]{3,2,1,0:T(8,128)(2,1)} %c_ref.3, bf16[2,20,768]{2,1,0:T(8,128)(2,1)} %copy.24.raw_ref, f32[24,3]{1,0:T(8,128)} %pad.4.params_ref), custom_call_target="tpu_custom_call" | custom-call | tf_op jit(solution)/shard_map/totals/pallas_call | solution.py:317
  10.1 31.0 %carry.1.carry_ref = f32[2,128,1280]{2,1,0:T(8,128)} custom-call(bf16[2,128,1280]{2,1,0:T(8,128)(2,1)} %get-tuple-element.11.state_ref, bf16[2,16,128]{2,1,0:T(8,128)(2,1)} %get-tuple-element.12.log_ref), custom_call_target="tpu_custom_call" | custom-call | tf_op jit(solution)/shard_map/carry/pallas_call | solution.py:342
  41.1 18.9 %scan.3 = (bf16[768,1280]{1,0:T(8,128)(2,1)}, f32[768,1]{1,0:T(8,128)}) custom-call(s32[1]{0:T(128)} %bitcast.4.d_ref, bf16[2,768,1280]{2,1,0:T(8,128)(2,1)} %x_ref.5, bf16[2,768,1280]{2,1,0:T(8,128)(2,1)} %gate_ref.3, bf16[2,2,768,128]{3,2,1,0:T(8,128)(2,1)} %c_ref.3, bf16[2,2,768,128]{3,2,1,0:T(8,128)(2,1)} %c_ref.3, bf16[2,20,768]{2,1,0:T(8,128)(2,1)} %copy.24.raw_ref, ...), custom_call_target="tpu_custom_call" | custom-call | flops 5033164800 | bytes 9175040 | tf_op jit(solution)/shard_map/scan/pallas_call | solution.py:368
  59.9 0.7 collective-permute-start
  60.7 1.3 %collective-permute-start.1 = (f32[768,1]{1,0:T(8,128)}, f32[768,1]{1,0:T(8,128)S(1)}, u32[]{:S(2)}, u32[]{:S(2)}) collective-permute-start(f32[768,1]{1,0:T(8,128)} %get-tuple-element.16), channel_id=1, source_target_pairs={{0,1},{1,0},{2,3},{3,2},{4,5},{5,4},{6,7},{7,6},{8,9},{9,8},{10,11... | collective-permute-start | bytes 9224 | tf_op jit(solution)/shard_map/ppermute | solution.py:414
  62.0 18.1 %scan.2 = (bf16[768,1280]{1,0:T(8,128)(2,1)}, f32[768,1]{1,0:T(8,128)}) custom-call(s32[1]{0:T(128)} %bitcast.d_ref, bf16[2,768,1280]{2,1,0:T(8,128)(2,1)} %x_ref.5, bf16[2,768,1280]{2,1,0:T(8,128)(2,1)} %gate_ref.3, bf16[2,2,768,128]{3,2,1,0:T(8,128)(2,1)} %c_ref.3, bf16[2,2,768,128]{3,2,1,0:T(8,128)(2,1)} %c_ref.3, bf16[2,20,768]{2,1,0:T(8,128)(2,1)} %copy.24.raw_ref, ...), custom_call_target="tpu_custom_call" | custom-call | flops 5033164800 | bytes 9175040 | tf_op jit(solution)/shard_map/scan/pallas_call | solution.py:368
  80.1 34.0 %collective-permute-done.1 = f32[768,1]{1,0:T(8,128)S(1)} collective-permute-done((f32[768,1]{1,0:T(8,128)}, f32[768,1]{1,0:T(8,128)S(1)}, u32[]{:S(2)}, u32[]{:S(2)}) %collective-permute-start.1) | collective-permute-done | bytes 3104 | tf_op jit(solution)/shard_map/ppermute | solution.py:414
  114.1 1.2 rsqrt_reduce_fusion
  115.3 0.0 collective-permute-done
  115.3 3.4 %multiply_convert_fusion = bf16[768,1280]{1,0:T(8,128)(2,1)} fusion(bf16[768,1280]{1,0:T(8,128)(2,1)S(1)} %collective-permute-done, bf16[768,1280]{1,0:T(8,128)(2,1)} %get-tuple-element.13, f32[768]{0:T(1024)S(1)} %rsqrt_reduce_fusion), kind=kLoop, calls=%fused_computation | loop fusion | flops 4915200 | bytes 5901312 | tf_op jit(solution)/shard_map/convert_element_type | solution.py:426
Async XLA Ops:
  59.9 55.4 %collective-permute-start = (bf16[768,1280]{1,0:T(8,128)(2,1)}, bf16[768,1280]{1,0:T(8,128)(2,1)S(1)}, u32[]{:S(2)}, u32[]{:S(2)}) collective-permute-start(bf16[768,1280]{1,0:T(8,128)(2,1)} %get-tuple-element.14), channel_id=1, source_target_pairs={{0,1},{1,0},{2,3},{3,2},{4,5},{5,4},{6,7},{7,6},{8,9},{9,8},{10,11... | collective-permute-start | bytes 5898248 | tf_op jit(solution)/shard_map/ppermute | solution.py:413
  60.7 53.5 %collective-permute-start.1 = (f32[768,1]{1,0:T(8,128)}, f32[768,1]{1,0:T(8,128)S(1)}, u32[]{:S(2)}, u32[]{:S(2)}) collective-permute-start(f32[768,1]{1,0:T(8,128)} %get-tuple-element.16), channel_id=1, source_target_pairs={{0,1},{1,0},{2,3},{3,2},{4,5},{5,4},{6,7},{7,6},{8,9},{9,8},{10,11... | collective-permute-start | bytes 9224 | tf_op jit(solution)/shard_map/ppermute | solution.py:414

commit v2 on v1

--- a/solution.py
+++ b/solution.py
@@ -212,7 +212,7 @@
 
 def scan_kernel(
     width, d_ref, x_ref, gate_ref, b_ref, c_ref, raw_ref, params_ref, gain_ref, w_ref, carry_ref,
-    part_ref, square_ref, raw_scr, state_scr, summed,
+    part_ref, square_ref, state_ref, raw_scr, state_scr, summed,
 ):
     heads = raw_ref.shape[1]
     rows, channels = x_ref.shape[1:]
@@ -272,10 +272,16 @@
         )
         decay = jnp.where(backward, entry_decay[0:1, :], entry_decay[SUB - 1 :, :])
         state_scr[...] = state_scr[...] * decay + fresh
+
+    @pl.when(pl.program_id(0) == pl.num_programs(0) - 1)
+    def _():
+        state_ref[0] = state_scr[...]
+
     scanned = summed[...].astype(BF16).astype(F32)
     gate = gate_ref[0].astype(F32)
     gated = scanned * (gate / (1.0 + jnp.exp(-gate)))
-    square_ref[...] = jnp.sum(gated * gated, axis=1, keepdims=True)
+    squares = jnp.sum(gated * gated, axis=1, keepdims=True)
+    square_ref[0] = jnp.broadcast_to(squares, (rows, SUB)).T[:8, :]
     part = jnp.dot(
         (gated * gain_ref[...]).astype(BF16), w_ref[...], preferred_element_type=F32
     ).astype(BF16)
@@ -293,6 +299,17 @@
             part_ref[:, k * SUB : (k + 1) * SUB] = jnp.dot(
                 taken, flip, preferred_element_type=F32
             ).astype(BF16)
+
+
+def finish_kernel(inner, d_ref, own_ref, square_ref, part_ref, other_ref, out_ref):
+    rows = own_ref.shape[0]
+    total = square_ref[0] + other_ref[0]
+    scale = lax.rsqrt(total / inner + EPS)
+    scale = jnp.broadcast_to(scale[0:1, :], (SUB, rows)).T
+    for k in range(own_ref.shape[1] // SUB):
+        span = slice(k * SUB, (k + 1) * SUB)
+        summed = own_ref[:, span].astype(F32) + part_ref[:, span].astype(F32)
+        out_ref[:, span] = (summed * scale).astype(BF16)
 
 
 def per_device(
@@ -364,30 +381,42 @@
     def place(k, d):
         return k + d[0] * (blocks - 1 - 2 * k)
 
-    def scan(d):
+    def scan(d, first, count, entering, pick):
+        whole = count == blocks
+
+        def at(k, d):
+            return place(first + k, d)
+
+        def to(k, d):
+            return place(k, d) if whole else k
+
         return pl.pallas_call(
             functools.partial(scan_kernel, width),
             out_shape=(
-                jax.ShapeDtypeStruct((tokens, half), BF16),
-                jax.ShapeDtypeStruct((tokens, 1), F32),
+                jax.ShapeDtypeStruct((count * block, half), BF16),
+                jax.ShapeDtypeStruct((count, 8, block), F32),
+                jax.ShapeDtypeStruct((1, state, channels), F32),
             ),
             grid_spec=pltpu.PrefetchScalarGridSpec(
                 num_scalar_prefetch=1,
-                grid=(blocks,),
+                grid=(count,),
                 in_specs=[
-                    pl.BlockSpec((1, block, channels), lambda k, d: (d[0], place(k, d), 0)),
-                    pl.BlockSpec((1, block, channels), lambda k, d: (d[0], place(k, d), 0)),
-                    pl.BlockSpec((1, 1, block, state), lambda k, d: (d[0], 0, place(k, d), 0)),
-                    pl.BlockSpec((1, 1, block, state), lambda k, d: (d[0], 1, place(k, d), 0)),
-                    pl.BlockSpec((1, heads, block), lambda k, d: (d[0], 0, place(k, d))),
+                    pl.BlockSpec((1, block, channels), lambda k, d: (d[0], at(k, d), 0)),
+                    pl.BlockSpec((1, block, channels), lambda k, d: (d[0], at(k, d), 0)),
+                    pl.BlockSpec((1, 1, block, state), lambda k, d: (d[0], 0, at(k, d), 0)),
+                    pl.BlockSpec((1, 1, block, state), lambda k, d: (d[0], 1, at(k, d), 0)),
+                    pl.BlockSpec((1, heads, block), lambda k, d: (d[0], 0, at(k, d))),
                     pl.BlockSpec((head_rows, 3), lambda k, d: (0, 0)),
                     pl.BlockSpec((1, channels), lambda k, d: (0, 0)),
                     pl.BlockSpec((channels, half), lambda k, d: (0, 0)),
-                    pl.BlockSpec((1, state, channels), lambda k, d: (d[0], 0, 0)),
+                    pl.BlockSpec(
+                        (1, state, channels), lambda k, d: (d[0] if pick else 0, 0, 0)
+                    ),
                 ],
                 out_specs=[
-                    pl.BlockSpec((block, half), lambda k, d: (place(k, d), 0)),
-                    pl.BlockSpec((block, 1), lambda k, d: (place(k, d), 0)),
+                    pl.BlockSpec((block, half), lambda k, d: (to(k, d), 0)),
+                    pl.BlockSpec((1, 8, block), lambda k, d: (to(k, d), 0, 0)),
+                    pl.BlockSpec((1, state, channels), lambda k, d: (0, 0, 0)),
                 ],
                 scratch_shapes=[
                     pltpu.VMEM((head_rows, block), F32),
@@ -396,33 +425,58 @@
                 ],
             ),
             cost_estimate=pl.CostEstimate(
-                flops=4 * tokens * channels * half,
-                bytes_accessed=6 * tokens * channels + 2 * channels * half,
+                flops=8 * count * block * channels * half,
+                bytes_accessed=6 * count * block * channels + 2 * channels * half,
                 transcendentals=0,
             ),
             name="scan",
         )(
             d.astype(jnp.int32).reshape(1), channels_in, gate_in, projections, projections,
-            step_raw, params, norm_gain[None], out_weight, carries,
-        )
+            step_raw, params, norm_gain[None], out_weight, entering,
+        )
+
+    def finish(d, k, own, squares, part, others):
+        return pl.pallas_call(
+            functools.partial(finish_kernel, inner),
+            out_shape=jax.ShapeDtypeStruct(own.shape, BF16),
+            grid_spec=pltpu.PrefetchScalarGridSpec(
+                num_scalar_prefetch=1,
+                grid=(1,),
+                in_specs=[
+                    pl.BlockSpec((block, half), lambda i, d: (place(k, d), 0)),
+                    pl.BlockSpec((1, 8, block), lambda i, d: (place(k, d), 0, 0)),
+                    pl.BlockSpec((block, half), lambda i, d: (0, 0)),
+                    pl.BlockSpec((1, 8, block), lambda i, d: (0, 0, 0)),
+                ],
+                out_specs=pl.BlockSpec((block, half), lambda i, d: (place(k, d), 0)),
+            ),
+            input_output_aliases={1: 0},
+            cost_estimate=pl.CostEstimate(
+                flops=4 * block * half, bytes_accessed=6 * block * half, transcendentals=0
+            ),
+            name="finish",
+        )(d.astype(jnp.int32).reshape(1), own, squares, part, others)
 
     group = lax.axis_index("head")
     if groups == 2:
         swap = [(0, 1), (1, 0)]
-        part, square = scan(1 - group)
-        part = lax.ppermute(part, "head", swap)
-        square = lax.ppermute(square, "head", swap)
-        own_part, own_square = scan(group)
-        summed = own_part.astype(F32) + part.astype(F32)
-        squares = own_square + square
-    else:
-        results = [scan(jnp.asarray(d)) for d in range(2)]
-        summed = lax.psum_scatter(
-            jnp.concatenate([results[0][0], results[1][0]], axis=1),
-            "head", scatter_dimension=1, tiled=True,
-        ).astype(F32)
-        both = lax.psum(jnp.stack([results[0][1], results[1][1]]), "head")
-        squares = jnp.where(2 * group >= groups, both[1], both[0])
+        arrived = []
+        entering, pick = carries, True
+        for k in range(blocks):
+            part, squares, entering = scan(1 - group, k, 1, entering, pick)
+            pick = False
+            arrived.append((lax.ppermute(part, "head", swap), lax.ppermute(squares, "head", swap)))
+        own, squares, _ = scan(group, 0, blocks, carries, True)
+        for k, (part, others) in enumerate(arrived):
+            own = finish(group, k, own, squares, part, others)
+        return own
+    results = [scan(jnp.asarray(d), 0, blocks, carries, True) for d in range(2)]
+    summed = lax.psum_scatter(
+        jnp.concatenate([results[0][0], results[1][0]], axis=1),
+        "head", scatter_dimension=1, tiled=True,
+    ).astype(F32)
+    both = lax.psum(jnp.stack([results[0][1][:, 0], results[1][1][:, 0]]), "head")
+    squares = jnp.where(2 * group >= groups, both[1], both[0]).reshape(tokens, 1)
     return (summed * lax.rsqrt(squares / inner + EPS)).astype(BF16)
 
 

time: 119 us -> 102 us (0.86)
  waiting for transfers between devices: 34 us -> 0.02 us
  Pallas kernels: 73.9 us -> 87.2 us
  other arithmetic: 5.29 us -> 0.7 us
  starting transfers between devices: 2.03 us -> 6.08 us
  local copies, waits for them, and re-layouts: 3.46 us -> 7.18 us
    ppermute x2 -> x6, waiting for transfers between devices: 34 us -> 0.02 us  [the longest x3 0.01 us: per_device(): lax.ppermute(part, 'head', swap)]
    pallas_call x0 -> x3, Pallas kernels: none -> 7.11 us  [finish(): pl.pallas_call(functools.partial(finish_kernel, inner), out_shape=jax.Sha...]
    pallas_call x2 -> x4, Pallas kernels: 37 us -> 43.4 us  [scan(): pl.pallas_call(functools.partial(scan_kernel, width), out_shape=(jax.Shap...]
    ppermute x2 -> x6, starting transfers between devices: 2.03 us -> 6.08 us  [the longest x3 3.09 us: per_device(): lax.ppermute(squares, 'head', swap)]
    unnamed x1 -> x13, local copies, waits for them, and re-layouts: 1.47 us -> 5.19 us
    convert_element_type x1 -> x0, other arithmetic: 3.41 us -> none  [per_device(): return (summed * lax.rsqrt(squares / inner + EPS)).astype(BF16)]
  transfers between devices with their start and end apart: 2 -> 6, of which waited for: 1 -> 0; matrix products, arithmetic and copies ran while one was open for 1% -> 0% of each run, Pallas kernels for 15% -> 39%
where the time goes in v2:
time: 102 us; the launch traced here: 101 us
  Pallas kernels  87.2 us (85%)
  local copies, waits for them, and re-layouts  7.18 us (7%)
  starting transfers between devices  6.08 us (6%)
    pallas_call x4, Pallas kernels, scan(): pl.pallas_call(functools.partial(scan_kernel, width), out_shape=(jax.Shap...  43.4 us
    pallas_call x1, Pallas kernels, per_device(): pl.pallas_call(functools.partial(carry_kernel, width, mates, planes), out...  30.8 us
    pallas_call x3, Pallas kernels, finish(): pl.pallas_call(functools.partial(finish_kernel, inner), out_shape=jax.Sha...  7.11 us
    pallas_call x1, Pallas kernels, per_device(): pl.pallas_call(functools.partial(totals_kernel, width), out_shape=(jax.Sh...  5.93 us
    unnamed x13, local copies, waits for them, and re-layouts  5.19 us
    ppermute x3, starting transfers between devices, per_device(): lax.ppermute(squares, 'head', swap)  3.09 us
    ppermute x3, starting transfers between devices, per_device(): lax.ppermute(part, 'head', swap)  2.99 us
  transfers between devices with their start and end apart: 6, of which 0 were waited for; matrix products, arithmetic and copies ran while one was open for 0% of the time, Pallas kernels for 39%

profile of v2, /device:TPU:0, one launch (start us, length us, event | category | flops | bytes accessed | tf_op | source)
XLA Modules:
  0.0 101.3 jit_solution(10400064324602804252)
XLA Ops:
  0.0 1.5 %copy.23.raw_ref = bf16[2,20,768]{2,1,0:T(8,128)(2,1)} copy(bf16[2,20,768]{2,0,1:T(2,128)(2,1)} %param.12) | data formatting | bytes 122880 | tf_op args[3]
  1.5 0.7 pad_maximum_fusion
  2.2 0.1 copy.21
  2.3 1.3 %broadcast_in_dim.2.gain_ref = f32[1,1280]{1,0:T(1,128)} reshape(f32[1280]{0:T(1024)} %param.16) | data formatting | bytes 10240 | tf_op jit(solution)/shard_map/broadcast_in_dim | solution.py:435
  3.6 0.6 pad.4.params_ref
  4.2 5.9 %totals.1 = (bf16[2,128,1280]{2,1,0:T(8,128)(2,1)}, bf16[2,16,128]{2,1,0:T(8,128)(2,1)}) custom-call(bf16[2,768,1280]{2,1,0:T(8,128)(2,1)} %x_ref.9, bf16[2,2,768,128]{3,2,1,0:T(8,128)(2,1)} %c_ref.7, bf16[2,20,768]{2,1,0:T(8,128)(2,1)} %copy.23.raw_ref, f32[24,3]{1,0:T(8,128)} %pad.4.params_ref), custom_call_target="tpu_custom_call" | custom-call | tf_op jit(solution)/shard_map/totals/pallas_call | solution.py:334
  10.1 30.8 %carry.1.carry_ref = f32[2,128,1280]{2,1,0:T(8,128)} custom-call(bf16[2,128,1280]{2,1,0:T(8,128)(2,1)} %get-tuple-element.17.state_ref, bf16[2,16,128]{2,1,0:T(8,128)(2,1)} %get-tuple-element.18.log_ref), custom_call_target="tpu_custom_call" | custom-call | tf_op jit(solution)/shard_map/carry/pallas_call | solution.py:359
  40.9 8.5 %scan.5 = (bf16[256,1280]{1,0:T(8,128)(2,1)}, f32[1,8,256]{2,1,0:T(8,128)}, f32[1,128,1280]{2,1,0:T(8,128)}) custom-call(s32[1]{0:T(128)} %bitcast.4.d_ref, bf16[2,768,1280]{2,1,0:T(8,128)(2,1)} %x_ref.9, bf16[2,768,1280]{2,1,0:T(8,128)(2,1)} %gate_ref.7, bf16[2,2,768,128]{3,2,1,0:T(8,128)(2,1)} %c_ref.7, bf16[2,2,768,128]{3,2,1,0:T(8,128)(2,1)} %c_ref.7, ...), custom_call_target="tpu_custom_call" | custom-call | flops 3355443200 | bytes 5242880 | tf_op jit(solution)/shard_map/scan/pallas_call | solution.py:393
  49.4 1.3 %collective-permute-start = (bf16[256,1280]{1,0:T(8,128)(2,1)}, bf16[256,1280]{1,0:T(8,128)(2,1)S(1)}, u32[]{:S(2)}, u32[]{:S(2)}) collective-permute-start(bf16[256,1280]{1,0:T(8,128)(2,1)} %get-tuple-element.21), channel_id=1, source_target_pairs={{0,1},{1,0},{2,3},{3,2},{4,5},{5,4},{6,7},{7,6},{8,9},{9,8},{10,11... | collective-permute-start | bytes 1966088 | tf_op jit(solution)/shard_map/ppermute | solution.py:468
  50.7 0.8 collective-permute-start.1
  51.4 8.7 %scan.6 = (bf16[256,1280]{1,0:T(8,128)(2,1)}, f32[1,8,256]{2,1,0:T(8,128)}, f32[1,128,1280]{2,1,0:T(8,128)}) custom-call(s32[1]{0:T(128)} %bitcast.4.d_ref, bf16[2,768,1280]{2,1,0:T(8,128)(2,1)} %x_ref.9, bf16[2,768,1280]{2,1,0:T(8,128)(2,1)} %gate_ref.7, bf16[2,2,768,128]{3,2,1,0:T(8,128)(2,1)} %c_ref.7, bf16[2,2,768,128]{3,2,1,0:T(8,128)(2,1)} %c_ref.7, ...), custom_call_target="tpu_custom_call" | custom-call | flops 3355443200 | bytes 5242880 | tf_op jit(solution)/shard_map/scan/pallas_call | solution.py:393
  60.1 1.0 collective-permute-start.2
  61.1 1.0 %collective-permute-start.3 = (f32[1,8,256]{2,1,0:T(8,128)}, f32[1,8,256]{2,1,0:T(8,128)S(1)}, u32[]{:S(2)}, u32[]{:S(2)}) collective-permute-start(f32[1,8,256]{2,1,0:T(8,128)} %get-tuple-element.25), channel_id=1, source_target_pairs={{0,1},{1,0},{2,3},{3,2},{4,5},{5,4},{6,7},{7,6},{8,9},{9,8},{10,11... | collective-permute-start | bytes 24584 | tf_op jit(solution)/shard_map/ppermute | solution.py:468
  62.2 8.5 %scan.7 = (bf16[256,1280]{1,0:T(8,128)(2,1)}, f32[1,8,256]{2,1,0:T(8,128)}, f32[1,128,1280]{2,1,0:T(8,128)}) custom-call(s32[1]{0:T(128)} %bitcast.4.d_ref, bf16[2,768,1280]{2,1,0:T(8,128)(2,1)} %x_ref.9, bf16[2,768,1280]{2,1,0:T(8,128)(2,1)} %gate_ref.7, bf16[2,2,768,128]{3,2,1,0:T(8,128)(2,1)} %c_ref.7, bf16[2,2,768,128]{3,2,1,0:T(8,128)(2,1)} %c_ref.7, ...), custom_call_target="tpu_custom_call" | custom-call | flops 3355443200 | bytes 5242880 | tf_op jit(solution)/shard_map/scan/pallas_call | solution.py:393
  70.7 0.7 collective-permute-start.4
  71.4 0.0 collective-permute-done.1.other_ref
  71.4 0.0 copy-start.3
  71.4 1.3 %collective-permute-start.5 = (f32[1,8,256]{2,1,0:T(8,128)}, f32[1,8,256]{2,1,0:T(8,128)S(1)}, u32[]{:S(2)}, u32[]{:S(2)}) collective-permute-start(f32[1,8,256]{2,1,0:T(8,128)} %get-tuple-element.28), channel_id=1, source_target_pairs={{0,1},{1,0},{2,3},{3,2},{4,5},{5,4},{6,7},{7,6},{8,9},{9,8},{10,11... | collective-permute-start | bytes 24584 | tf_op jit(solution)/shard_map/ppermute | solution.py:468
  72.7 17.7 %scan.4 = (bf16[768,1280]{1,0:T(8,128)(2,1)}, f32[3,8,256]{2,1,0:T(8,128)}, f32[1,128,1280]{2,1,0:T(8,128)}) custom-call(s32[1]{0:T(128)} %bitcast.d_ref, bf16[2,768,1280]{2,1,0:T(8,128)(2,1)} %x_ref.9, bf16[2,768,1280]{2,1,0:T(8,128)(2,1)} %gate_ref.7, bf16[2,2,768,128]{3,2,1,0:T(8,128)(2,1)} %c_ref.7, bf16[2,2,768,128]{3,2,1,0:T(8,128)(2,1)} %c_ref.7, ...), custom_call_target="tpu_custom_call" | custom-call | flops 10066329600 | bytes 9175040 | tf_op jit(solution)/shard_map/scan/pallas_call | solution.py:393
  90.4 0.0 copy-done.3
  90.4 0.0 collective-permute-done.part_ref
  90.4 0.0 copy-start
  90.4 0.8 copy-done
  91.3 2.4 %finish.3.own_ref = bf16[768,1280]{1,0:T(8,128)(2,1)} custom-call(s32[1]{0:T(128)} %bitcast.d_ref, bf16[768,1280]{1,0:T(8,128)(2,1)} %get-tuple-element.19.own_ref, f32[3,8,256]{2,1,0:T(8,128)} %get-tuple-element.20.square_ref, bf16[256,1280]{1,0:T(8,128)(2,1)} %copy-done, f32[1,8,256]{2,1,0:T(8,128)} %copy-done.3), custom_call_target="tpu_custom_call", output_to_operand_aliasing={{}: (1, {})} | custom-call | flops 1310720 | bytes 1966080 | tf_op jit(solution)/shard_map/finish/pallas_call | solution.py:439
  93.7 0.0 collective-permute-done.3.other_ref
  93.7 0.0 copy-start.4
  93.7 0.0 collective-permute-done.2.part_ref
  93.7 0.6 copy-done.4
  94.2 0.0 copy-start.1
  94.2 0.8 copy-done.1
  95.1 2.4 %finish.4.own_ref = bf16[768,1280]{1,0:T(8,128)(2,1)} custom-call(s32[1]{0:T(128)} %bitcast.d_ref, bf16[768,1280]{1,0:T(8,128)(2,1)} %finish.3.own_ref, f32[3,8,256]{2,1,0:T(8,128)} %get-tuple-element.20.square_ref, bf16[256,1280]{1,0:T(8,128)(2,1)} %copy-done.1, f32[1,8,256]{2,1,0:T(8,128)} %copy-done.4), custom_call_target="tpu_custom_call", output_to_operand_aliasing={{}: (1, {})} | custom-call | flops 1310720 | bytes 1966080 | tf_op jit(solution)/shard_map/finish/pallas_call | solution.py:439
  97.5 0.0 collective-permute-done.5.other_ref
  97.5 0.0 copy-start.5
  97.5 0.0 collective-permute-done.4.part_ref
  97.5 0.6 copy-done.5
  98.1 0.0 copy-start.2
  98.1 0.8 copy-done.2
  98.9 2.4 %finish.5 = bf16[768,1280]{1,0:T(8,128)(2,1)} custom-call(s32[1]{0:T(128)} %bitcast.d_ref, bf16[768,1280]{1,0:T(8,128)(2,1)} %finish.4.own_ref, f32[3,8,256]{2,1,0:T(8,128)} %get-tuple-element.20.square_ref, bf16[256,1280]{1,0:T(8,128)(2,1)} %copy-done.2, f32[1,8,256]{2,1,0:T(8,128)} %copy-done.5), custom_call_target="tpu_custom_call", output_to_operand_aliasing={{}: (1, {})} | custom-call | flops 1310720 | bytes 1966080 | tf_op jit(solution)/shard_map/finish/pallas_call | solution.py:439
Async XLA Ops:
  49.4 41.0 %collective-permute-start = (bf16[256,1280]{1,0:T(8,128)(2,1)}, bf16[256,1280]{1,0:T(8,128)(2,1)S(1)}, u32[]{:S(2)}, u32[]{:S(2)}) collective-permute-start(bf16[256,1280]{1,0:T(8,128)(2,1)} %get-tuple-element.21), channel_id=1, source_target_pairs={{0,1},{1,0},{2,3},{3,2},{4,5},{5,4},{6,7},{7,6},{8,9},{9,8},{10,11... | collective-permute-start | bytes 1966088 | tf_op jit(solution)/shard_map/ppermute | solution.py:468
  50.7 20.8 %collective-permute-start.1 = (f32[1,8,256]{2,1,0:T(8,128)}, f32[1,8,256]{2,1,0:T(8,128)S(1)}, u32[]{:S(2)}, u32[]{:S(2)}) collective-permute-start(f32[1,8,256]{2,1,0:T(8,128)} %get-tuple-element.22), channel_id=1, source_target_pairs={{0,1},{1,0},{2,3},{3,2},{4,5},{5,4},{6,7},{7,6},{8,9},{9,8},{10,11... | collective-permute-start | bytes 24584 | tf_op jit(solution)/shard_map/ppermute | solution.py:468
  60.1 33.5 %collective-permute-start.2 = (bf16[256,1280]{1,0:T(8,128)(2,1)}, bf16[256,1280]{1,0:T(8,128)(2,1)S(1)}, u32[]{:S(2)}, u32[]{:S(2)}) collective-permute-start(bf16[256,1280]{1,0:T(8,128)(2,1)} %get-tuple-element.24), channel_id=1, source_target_pairs={{0,1},{1,0},{2,3},{3,2},{4,5},{5,4},{6,7},{7,6},{8,9},{9,8},{10,11... | collective-permute-start | bytes 1966088 | tf_op jit(solution)/shard_map/ppermute | solution.py:468
  61.1 32.5 %collective-permute-start.3 = (f32[1,8,256]{2,1,0:T(8,128)}, f32[1,8,256]{2,1,0:T(8,128)S(1)}, u32[]{:S(2)}, u32[]{:S(2)}) collective-permute-start(f32[1,8,256]{2,1,0:T(8,128)} %get-tuple-element.25), channel_id=1, source_target_pairs={{0,1},{1,0},{2,3},{3,2},{4,5},{5,4},{6,7},{7,6},{8,9},{9,8},{10,11... | collective-permute-start | bytes 24584 | tf_op jit(solution)/shard_map/ppermute | solution.py:468
  70.7 26.8 %collective-permute-start.4 = (bf16[256,1280]{1,0:T(8,128)(2,1)}, bf16[256,1280]{1,0:T(8,128)(2,1)S(1)}, u32[]{:S(2)}, u32[]{:S(2)}) collective-permute-start(bf16[256,1280]{1,0:T(8,128)(2,1)} %get-tuple-element.27), channel_id=1, source_target_pairs={{0,1},{1,0},{2,3},{3,2},{4,5},{5,4},{6,7},{7,6},{8,9},{9,8},{10,11... | collective-permute-start | bytes 1966088 | tf_op jit(solution)/shard_map/ppermute | solution.py:468
  71.4 19.0 %copy-start.3 = (f32[1,8,256]{2,1,0:T(8,128)}, f32[1,8,256]{2,1,0:T(8,128)S(1)}, u32[]{:S(2)}) copy-start(f32[1,8,256]{2,1,0:T(8,128)S(1)} %collective-permute-done.1.other_ref) | copy-start | bytes 24580
  71.4 26.0 %collective-permute-start.5 = (f32[1,8,256]{2,1,0:T(8,128)}, f32[1,8,256]{2,1,0:T(8,128)S(1)}, u32[]{:S(2)}, u32[]{:S(2)}) collective-permute-start(f32[1,8,256]{2,1,0:T(8,128)} %get-tuple-element.28), channel_id=1, source_target_pairs={{0,1},{1,0},{2,3},{3,2},{4,5},{5,4},{6,7},{7,6},{8,9},{9,8},{10,11... | collective-permute-start | bytes 24584 | tf_op jit(solution)/shard_map/ppermute | solution.py:468
  90.4 0.8 copy-start
  93.7 0.6 copy-start.4
  94.2 0.8 copy-start.1
  97.5 0.6 copy-start.5
  98.1 0.8 copy-start.2

commit v3 on v2

--- a/solution.py
+++ b/solution.py
@@ -97,12 +97,13 @@
 
 
 def carry_kernel(
-    width, mates, planes, state_ref, log_ref, out_ref, one_state, one_log, sum_state, sum_log,
+    width, mates, planes, turns, state_ref, log_ref, out_ref, one_state, one_log, sum_state, sum_log,
     two_state, two_log, entry, mine, three_state, send_sem, recv_sem,
 ):
     device = lax.axis_index("seq")
     plane, spot = device // mates, device % mates
-    rows = one_state.shape[2]
+    rows = one_state.shape[3]
+    span = 3 * mates + 2 * planes
     channels = state_ref.shape[-1]
     matrix = spreader(SUB, channels, width)[:SUB]
 
@@ -113,8 +114,8 @@
             device_id_type=pl.DeviceIdType.MESH,
         )
 
-    def rows_of(q):
-        return pl.ds(pl.multiple_of(q * rows, rows), rows)
+    def rows_of(q, turn):
+        return pl.ds(pl.multiple_of((q * turns + turn) * rows, rows), rows)
 
     def decay_of(packed):
         both = jnp.dot(packed, matrix, preferred_element_type=F32)
@@ -135,77 +136,105 @@
         )
     pl.semaphore_wait(barrier, mates + planes - 2)
 
-    base = 0
+    orders = [list(range(mates)), list(range(mates))[::-1]]
     started = []
-    for o, q in enumerate(others):
-        to = plane * mates + q
-        started.append(
-            remote(state_ref.at[:, rows_of(q)], one_state.at[spot], base + 2 * o, base + 2 * spot, to)
-        )
-        started.append(
-            remote(log_ref, one_log.at[spot], base + 2 * o + 1, base + 2 * spot + 1, to)
-        )
-    for copy in started:
-        copy.start()
-    one_state[spot] = state_ref[:, rows_of(spot), :]
-    one_log[spot] = log_ref[...]
-    for o, q in enumerate(others):
-        remote(one_state.at[q], one_state.at[q], base + 2 * o, base + 2 * q, device).wait_recv()
-        remote(one_log.at[q], one_log.at[q], base + 2 * o + 1, base + 2 * q + 1, device).wait_recv()
-
-    decays = [[decay_of(one_log[q, d]) for q in range(mates)] for d in range(2)]
-    orders = [list(range(mates)), list(range(mates))[::-1]]
-    for d in range(2):
-        total = None
-        logs = None
-        for q in orders[d]:
-            part = one_state[q, d].astype(F32)
-            log = one_log[q, d].astype(F32)
-            total = part if total is None else total * decays[d][q] + part
-            logs = log if logs is None else logs + log
-        sum_state[d] = total.astype(BF16)
-        sum_log[d] = packed_row(logs[0:1, :] + logs[1:2, :])
-    base = 2 * mates
-    for o, p in enumerate(far):
-        d = jnp.where(p > plane, 0, 1)
-        to = p * mates + spot
-        for j, (source, target) in enumerate(((sum_state, two_state), (sum_log, two_log))):
-            copy = remote(
-                source.at[d], target.at[plane], base + 2 * o + j, base + 2 * plane + j, to
-            )
-            copy.start()
-            started.append(copy)
-    for o, p in enumerate(far):
-        for j, target in enumerate((two_state, two_log)):
-            remote(
-                target.at[p], target.at[p], base + 2 * o + j, base + 2 * p + j, device
-            ).wait_recv()
-    entry[...] = jnp.zeros_like(entry)
-
-    def link(d, p):
-        entry[d] = entry[d] * decay_of(two_log[p]) + two_state[p].astype(F32)
-
-    for p in range(planes):
-        pl.when(p < plane)(functools.partial(link, 0, p))
-        pl.when(planes - 1 - p > plane)(functools.partial(link, 1, planes - 1 - p))
-
-    base = 2 * mates + 2 * planes
-    for d in range(2):
-        carried = entry[d]
-        for q in orders[d]:
-            mine[q, d] = carried.astype(BF16)
-            if q != orders[d][-1]:
-                carried = carried * decays[d][q] + one_state[q, d].astype(F32)
-    for o, q in enumerate(others):
-        copy = remote(mine.at[q], three_state.at[spot], base + o, base + spot, plane * mates + q)
+
+    def begin(copy):
         copy.start()
         started.append(copy)
-    three_state[spot] = mine[spot]
-    for o, q in enumerate(others):
-        remote(three_state.at[q], three_state.at[q], base + o, base + q, device).wait_recv()
-    for q in range(mates):
+
+    for turn in range(turns):
+        base = turn * span
+        for o, q in enumerate(others):
+            to = plane * mates + q
+            begin(
+                remote(
+                    state_ref.at[:, rows_of(q, turn)], one_state.at[turn, spot], base + 2 * o,
+                    base + 2 * spot, to,
+                )
+            )
+            if turn == 0:
+                begin(remote(log_ref, one_log.at[spot], 2 * o + 1, 2 * spot + 1, to))
+        one_state[turn, spot] = state_ref[:, rows_of(spot, turn), :]
+    one_log[spot] = log_ref[...]
+
+    for turn in range(turns):
+        base = turn * span
+        for o, q in enumerate(others):
+            target = one_state.at[turn, q]
+            remote(target, target, base + 2 * o, base + 2 * q, device).wait_recv()
+            if turn == 0:
+                remote(one_log.at[q], one_log.at[q], 2 * o + 1, 2 * q + 1, device).wait_recv()
+        if turn == 0:
+            decays = [[decay_of(one_log[q, d]) for q in range(mates)] for d in range(2)]
         for d in range(2):
-            out_ref[d, q * rows : (q + 1) * rows, :] = three_state[q, d].astype(F32)
+            total = None
+            logs = None
+            for q in orders[d]:
+                part = one_state[turn, q, d].astype(F32)
+                log = one_log[q, d].astype(F32)
+                total = part if total is None else total * decays[d][q] + part
+                logs = log if logs is None else logs + log
+            sum_state[turn, d] = total.astype(BF16)
+            if turn == 0:
+                sum_log[d] = packed_row(logs[0:1, :] + logs[1:2, :])
+        base = turn * span + 2 * mates
+        for o, p in enumerate(far):
+            d = jnp.where(p > plane, 0, 1)
+            to = p * mates + spot
+            begin(
+                remote(
+                    sum_state.at[turn, d], two_state.at[turn, plane], base + 2 * o,
+                    base + 2 * plane, to,
+                )
+            )
+            if turn == 0:
+                begin(
+                    remote(
+                        sum_log.at[d], two_log.at[plane], base + 2 * o + 1, base + 2 * plane + 1, to
+                    )
+                )
+
+    def link(turn, d, p):
+        entry[turn, d] = entry[turn, d] * decay_of(two_log[p]) + two_state[turn, p].astype(F32)
+
+    entry[...] = jnp.zeros_like(entry)
+    for turn in range(turns):
+        base = turn * span + 2 * mates
+        for o, p in enumerate(far):
+            target = two_state.at[turn, p]
+            remote(target, target, base + 2 * o, base + 2 * p, device).wait_recv()
+            if turn == 0:
+                target = two_log.at[p]
+                remote(target, target, base + 2 * o + 1, base + 2 * p + 1, device).wait_recv()
+        for p in range(planes):
+            last = planes - 1 - p
+            pl.when(p < plane)(functools.partial(link, turn, 0, p))
+            pl.when(last > plane)(functools.partial(link, turn, 1, last))
+        base = turn * span + 2 * mates + 2 * planes
+        for d in range(2):
+            carried = entry[turn, d]
+            for q in orders[d]:
+                mine[turn, q, d] = carried.astype(BF16)
+                if q != orders[d][-1]:
+                    carried = carried * decays[d][q] + one_state[turn, q, d].astype(F32)
+        for o, q in enumerate(others):
+            begin(
+                remote(
+                    mine.at[turn, q], three_state.at[turn, spot], base + o, base + spot,
+                    plane * mates + q,
+                )
+            )
+        three_state[turn, spot] = mine[turn, spot]
+    for turn in range(turns):
+        base = turn * span + 2 * mates + 2 * planes
+        for o, q in enumerate(others):
+            target = three_state.at[turn, q]
+            remote(target, target, base + o, base + q, device).wait_recv()
+        for q in range(mates):
+            at = (q * turns + turn) * rows
+            for d in range(2):
+                out_ref[d, at : at + rows, :] = three_state[turn, q, d].astype(F32)
     for copy in started:
         copy.wait_send()
 
@@ -301,15 +330,22 @@
             ).astype(BF16)
 
 
-def finish_kernel(inner, d_ref, own_ref, square_ref, part_ref, other_ref, out_ref):
+def finish_kernel(inner, count, d_ref, own_ref, square_ref, *refs):
+    out_ref = refs[-1]
     rows = own_ref.shape[0]
-    total = square_ref[0] + other_ref[0]
-    scale = lax.rsqrt(total / inner + EPS)
-    scale = jnp.broadcast_to(scale[0:1, :], (SUB, rows)).T
-    for k in range(own_ref.shape[1] // SUB):
-        span = slice(k * SUB, (k + 1) * SUB)
-        summed = own_ref[:, span].astype(F32) + part_ref[:, span].astype(F32)
-        out_ref[:, span] = (summed * scale).astype(BF16)
+
+    def finish(part_ref, other_ref):
+        total = square_ref[0] + other_ref[0]
+        scale = lax.rsqrt(total / inner + EPS)
+        scale = jnp.broadcast_to(scale[0:1, :], (SUB, rows)).T
+        for k in range(own_ref.shape[1] // SUB):
+            span = slice(k * SUB, (k + 1) * SUB)
+            summed = own_ref[:, span].astype(F32) + part_ref[:, span].astype(F32)
+            out_ref[:, span] = (summed * scale).astype(BF16)
+
+    for i in range(count):
+        chosen = functools.partial(finish, refs[i], refs[count + i])
+        pl.when(pl.program_id(0) == i)(chosen)
 
 
 def per_device(
@@ -354,23 +390,24 @@
 
     mates = math.gcd(devices, 4)
     planes = devices // mates
-    share = state // mates
-    copies = 3 * mates + 2 * planes
+    turns = 2
+    share = state // mates // turns
+    copies = turns * (3 * mates + 2 * planes)
     carries = pl.pallas_call(
-        functools.partial(carry_kernel, width, mates, planes),
+        functools.partial(carry_kernel, width, mates, planes, turns),
         out_shape=jax.ShapeDtypeStruct((2, state, channels), F32),
         in_specs=[pl.BlockSpec(memory_space=pltpu.VMEM)] * 2,
         out_specs=pl.BlockSpec(memory_space=pltpu.VMEM),
         scratch_shapes=[
-            pltpu.VMEM((mates, 2, share, channels), BF16),
+            pltpu.VMEM((turns, mates, 2, share, channels), BF16),
             pltpu.VMEM((mates, 2, PAD, SUB), BF16),
-            pltpu.VMEM((2, share, channels), BF16),
+            pltpu.VMEM((turns, 2, share, channels), BF16),
             pltpu.VMEM((2, PAD, SUB), BF16),
-            pltpu.VMEM((planes, share, channels), BF16),
+            pltpu.VMEM((turns, planes, share, channels), BF16),
             pltpu.VMEM((planes, PAD, SUB), BF16),
-            pltpu.VMEM((2, share, channels), F32),
-            pltpu.VMEM((mates, 2, share, channels), BF16),
-            pltpu.VMEM((mates, 2, share, channels), BF16),
+            pltpu.VMEM((turns, 2, share, channels), F32),
+            pltpu.VMEM((turns, mates, 2, share, channels), BF16),
+            pltpu.VMEM((turns, mates, 2, share, channels), BF16),
             pltpu.SemaphoreType.DMA((copies,)),
             pltpu.SemaphoreType.DMA((copies,)),
         ],
@@ -435,27 +472,30 @@
             step_raw, params, norm_gain[None], out_weight, entering,
         )
 
-    def finish(d, k, own, squares, part, others):
+    def finish(d, first, arrived, own, squares):
+        count = len(arrived)
+        parts, others = zip(*arrived)
         return pl.pallas_call(
-            functools.partial(finish_kernel, inner),
+            functools.partial(finish_kernel, inner, count),
             out_shape=jax.ShapeDtypeStruct(own.shape, BF16),
             grid_spec=pltpu.PrefetchScalarGridSpec(
                 num_scalar_prefetch=1,
-                grid=(1,),
+                grid=(count,),
                 in_specs=[
-                    pl.BlockSpec((block, half), lambda i, d: (place(k, d), 0)),
-                    pl.BlockSpec((1, 8, block), lambda i, d: (place(k, d), 0, 0)),
-                    pl.BlockSpec((block, half), lambda i, d: (0, 0)),
-                    pl.BlockSpec((1, 8, block), lambda i, d: (0, 0, 0)),
+                    pl.BlockSpec((block, half), lambda i, d: (place(first + i, d), 0)),
+                    pl.BlockSpec((1, 8, block), lambda i, d: (place(first + i, d), 0, 0)),
+                    *[pl.BlockSpec((block, half), lambda i, d: (0, 0))] * count,
+                    *[pl.BlockSpec((1, 8, block), lambda i, d: (0, 0, 0))] * count,
                 ],
-                out_specs=pl.BlockSpec((block, half), lambda i, d: (place(k, d), 0)),
+                out_specs=pl.BlockSpec((block, half), lambda i, d: (place(first + i, d), 0)),
             ),
             input_output_aliases={1: 0},
             cost_estimate=pl.CostEstimate(
-                flops=4 * block * half, bytes_accessed=6 * block * half, transcendentals=0
+                flops=4 * count * block * half, bytes_accessed=6 * count * block * half,
+                transcendentals=0,
             ),
             name="finish",
-        )(d.astype(jnp.int32).reshape(1), own, squares, part, others)
+        )(d.astype(jnp.int32).reshape(1), own, squares, *parts, *others)
 
     group = lax.axis_index("head")
     if groups == 2:
@@ -467,9 +507,9 @@
             pick = False
             arrived.append((lax.ppermute(part, "head", swap), lax.ppermute(squares, "head", swap)))
         own, squares, _ = scan(group, 0, blocks, carries, True)
-        for k, (part, others) in enumerate(arrived):
-            own = finish(group, k, own, squares, part, others)
-        return own
+        if blocks > 1:
+            own = finish(group, 0, arrived[:-1], own, squares)
+        return finish(group, blocks - 1, arrived[-1:], own, squares)
     results = [scan(jnp.asarray(d), 0, blocks, carries, True) for d in range(2)]
     summed = lax.psum_scatter(
         jnp.concatenate([results[0][0], results[1][0]], axis=1),

time: 102 us -> 105 us (1.029)
  waiting for transfers between devices: 0.02 us -> 9.78 us
  Pallas kernels: 87.2 us -> 81.3 us
  local copies, waits for them, and re-layouts: 7.18 us -> 5.94 us
    ppermute x3, waiting for transfers between devices: 0.01 us -> 9.77 us  [per_device(): lax.ppermute(squares, 'head', swap)]
    pallas_call x4 -> x3, Pallas kernels: 37.9 us -> 31.9 us  [the longest x1 26.6 us: per_device(): pl.pallas_call(functools.partial(carry_kernel, width, mates, planes, turn...]
    unnamed x13 -> x15, local copies, waits for them, and re-layouts: 5.19 us -> 3.95 us
  transfers between devices with their start and end apart: 6 -> 6, of which waited for: 0 -> 1; matrix products, arithmetic and copies ran while one was open for 0% -> 0% of each run, Pallas kernels for 39% -> 36%
where the time goes in v3:
time: 105 us; the launch traced here: 104 us
  Pallas kernels  81.3 us (77%)
  waiting for transfers between devices  9.78 us (9%)
  starting transfers between devices  6.32 us (6%)
  local copies, waits for them, and re-layouts  5.94 us (6%)
    pallas_call x4, Pallas kernels, scan(): pl.pallas_call(functools.partial(scan_kernel, width), out_shape=(jax.Shap...  43.4 us
    pallas_call x1, Pallas kernels, per_device(): pl.pallas_call(functools.partial(carry_kernel, width, mates, planes, turn...  26.6 us
    ppermute x3, waiting for transfers between devices, per_device(): lax.ppermute(squares, 'head', swap)  9.77 us
    pallas_call x1, Pallas kernels, per_device(): pl.pallas_call(functools.partial(totals_kernel, width), out_shape=(jax.Sh...  5.94 us
    pallas_call x2, Pallas kernels, finish(): pl.pallas_call(functools.partial(finish_kernel, inner, count), out_shape=...  5.24 us
    unnamed x15, local copies, waits for them, and re-layouts  3.95 us
    ppermute x3, starting transfers between devices, per_device(): lax.ppermute(squares, 'head', swap)  3.3 us
    ppermute x3, starting transfers between devices, per_device(): lax.ppermute(part, 'head', swap)  3.01 us
  transfers between devices with their start and end apart: 6, of which 1 were waited for; matrix products, arithmetic and copies ran while one was open for 0% of the time, Pallas kernels for 36%

profile of v3, /device:TPU:0, one launch (start us, length us, event | category | flops | bytes accessed | tf_op | source)
XLA Modules:
  0.0 104.1 jit_solution(504182609780377597)
XLA Ops:
  0.0 1.5 %copy.22.raw_ref = bf16[2,20,768]{2,1,0:T(8,128)(2,1)} copy(bf16[2,20,768]{2,0,1:T(2,128)(2,1)} %param.12) | data formatting | bytes 122880 | tf_op args[3]
  1.5 0.7 pad_maximum_fusion
  2.2 0.1 copy.20
  2.3 1.3 %broadcast_in_dim.2.gain_ref = f32[1,1280]{1,0:T(1,128)} reshape(f32[1280]{0:T(1024)} %param.16) | data formatting | bytes 10240 | tf_op jit(solution)/shard_map/broadcast_in_dim | solution.py:472
  3.6 0.6 pad.4.params_ref
  4.2 5.9 %totals.1 = (bf16[2,128,1280]{2,1,0:T(8,128)(2,1)}, bf16[2,16,128]{2,1,0:T(8,128)(2,1)}) custom-call(bf16[2,768,1280]{2,1,0:T(8,128)(2,1)} %x_ref.9, bf16[2,2,768,128]{3,2,1,0:T(8,128)(2,1)} %c_ref.7, bf16[2,20,768]{2,1,0:T(8,128)(2,1)} %copy.22.raw_ref, f32[24,3]{1,0:T(8,128)} %pad.4.params_ref), custom_call_target="tpu_custom_call" | custom-call | tf_op jit(solution)/shard_map/totals/pallas_call | solution.py:370
  10.1 26.6 %carry.1.carry_ref = f32[2,128,1280]{2,1,0:T(8,128)} custom-call(bf16[2,128,1280]{2,1,0:T(8,128)(2,1)} %get-tuple-element.17.state_ref, bf16[2,16,128]{2,1,0:T(8,128)(2,1)} %get-tuple-element.18.log_ref), custom_call_target="tpu_custom_call" | custom-call | tf_op jit(solution)/shard_map/carry/pallas_call | solution.py:396
  36.8 8.5 %scan.5 = (bf16[256,1280]{1,0:T(8,128)(2,1)}, f32[1,8,256]{2,1,0:T(8,128)}, f32[1,128,1280]{2,1,0:T(8,128)}) custom-call(s32[1]{0:T(128)} %bitcast.4.d_ref, bf16[2,768,1280]{2,1,0:T(8,128)(2,1)} %x_ref.9, bf16[2,768,1280]{2,1,0:T(8,128)(2,1)} %gate_ref.7, bf16[2,2,768,128]{3,2,1,0:T(8,128)(2,1)} %c_ref.7, bf16[2,2,768,128]{3,2,1,0:T(8,128)(2,1)} %c_ref.7, ...), custom_call_target="tpu_custom_call" | custom-call | flops 3355443200 | bytes 5242880 | tf_op jit(solution)/shard_map/scan/pallas_call | solution.py:430
  45.3 1.3 %collective-permute-start = (bf16[256,1280]{1,0:T(8,128)(2,1)}, bf16[256,1280]{1,0:T(8,128)(2,1)S(1)}, u32[]{:S(2)}, u32[]{:S(2)}) collective-permute-start(bf16[256,1280]{1,0:T(8,128)(2,1)} %get-tuple-element.21), channel_id=1, source_target_pairs={{0,1},{1,0},{2,3},{3,2},{4,5},{5,4},{6,7},{7,6},{8,9},{9,8},{10,11... | collective-permute-start | bytes 1966088 | tf_op jit(solution)/shard_map/ppermute | solution.py:508
  46.5 0.0 copy-start.6
  46.5 8.7 %scan.6 = (bf16[256,1280]{1,0:T(8,128)(2,1)}, f32[1,8,256]{2,1,0:T(8,128)}, f32[1,128,1280]{2,1,0:T(8,128)}) custom-call(s32[1]{0:T(128)} %bitcast.4.d_ref, bf16[2,768,1280]{2,1,0:T(8,128)(2,1)} %x_ref.9, bf16[2,768,1280]{2,1,0:T(8,128)(2,1)} %gate_ref.7, bf16[2,2,768,128]{3,2,1,0:T(8,128)(2,1)} %c_ref.7, bf16[2,2,768,128]{3,2,1,0:T(8,128)(2,1)} %c_ref.7, ...), custom_call_target="tpu_custom_call" | custom-call | flops 3355443200 | bytes 5242880 | tf_op jit(solution)/shard_map/scan/pallas_call | solution.py:430
  55.2 0.5 collective-permute-start.1
  55.7 0.0 copy-done.6
  55.7 1.5 %collective-permute-start.2 = (f32[1,8,256]{2,1,0:T(8,128)S(1)}, f32[1,8,256]{2,1,0:T(8,128)S(1)}, u32[]{:S(2)}, u32[]{:S(2)}) collective-permute-start(f32[1,8,256]{2,1,0:T(8,128)S(1)} %copy-done.6), channel_id=1, source_target_pairs={{0,1},{1,0},{2,3},{3,2},{4,5},{5,4},{6,7},{7,6},{8,9},{9,8},{10,11... | collective-permute-start | bytes 24584 | tf_op jit(solution)/shard_map/ppermute | solution.py:508
  57.3 0.5 collective-permute-start.3
  57.8 8.5 %scan.7 = (bf16[256,1280]{1,0:T(8,128)(2,1)}, f32[1,8,256]{2,1,0:T(8,128)}, f32[1,128,1280]{2,1,0:T(8,128)}) custom-call(s32[1]{0:T(128)} %bitcast.4.d_ref, bf16[2,768,1280]{2,1,0:T(8,128)(2,1)} %x_ref.9, bf16[2,768,1280]{2,1,0:T(8,128)(2,1)} %gate_ref.7, bf16[2,2,768,128]{3,2,1,0:T(8,128)(2,1)} %c_ref.7, bf16[2,2,768,128]{3,2,1,0:T(8,128)(2,1)} %c_ref.7, ...), custom_call_target="tpu_custom_call" | custom-call | flops 3355443200 | bytes 5242880 | tf_op jit(solution)/shard_map/scan/pallas_call | solution.py:430
  66.3 1.3 %collective-permute-start.4 = (bf16[256,1280]{1,0:T(8,128)(2,1)}, bf16[256,1280]{1,0:T(8,128)(2,1)S(1)}, u32[]{:S(2)}, u32[]{:S(2)}) collective-permute-start(bf16[256,1280]{1,0:T(8,128)(2,1)} %get-tuple-element.27), channel_id=1, source_target_pairs={{0,1},{1,0},{2,3},{3,2},{4,5},{5,4},{6,7},{7,6},{8,9},{9,8},{10,11... | collective-permute-start | bytes 1966088 | tf_op jit(solution)/shard_map/ppermute | solution.py:508
  67.5 9.8 %collective-permute-done.2.refs_2_ = f32[1,8,256]{2,1,0:T(8,128)S(1)} collective-permute-done((f32[1,8,256]{2,1,0:T(8,128)S(1)}, f32[1,8,256]{2,1,0:T(8,128)S(1)}, u32[]{:S(2)}, u32[]{:S(2)}) %collective-permute-start.2) | collective-permute-done | bytes 8224 | tf_op jit(solution)/shard_map/ppermute | solution.py:508
  77.3 0.0 copy-start.3
  77.3 1.3 %collective-permute-start.5 = (f32[1,8,256]{2,1,0:T(8,128)}, f32[1,8,256]{2,1,0:T(8,128)S(1)}, u32[]{:S(2)}, u32[]{:S(2)}) collective-permute-start(f32[1,8,256]{2,1,0:T(8,128)} %get-tuple-element.28), channel_id=1, source_target_pairs={{0,1},{1,0},{2,3},{3,2},{4,5},{5,4},{6,7},{7,6},{8,9},{9,8},{10,11... | collective-permute-start | bytes 24584 | tf_op jit(solution)/shard_map/ppermute | solution.py:508
  78.6 17.7 %scan.4 = (bf16[768,1280]{1,0:T(8,128)(2,1)}, f32[3,8,256]{2,1,0:T(8,128)}, f32[1,128,1280]{2,1,0:T(8,128)}) custom-call(s32[1]{0:T(128)} %bitcast.d_ref, bf16[2,768,1280]{2,1,0:T(8,128)(2,1)} %x_ref.9, bf16[2,768,1280]{2,1,0:T(8,128)(2,1)} %gate_ref.7, bf16[2,2,768,128]{3,2,1,0:T(8,128)(2,1)} %c_ref.7, bf16[2,2,768,128]{3,2,1,0:T(8,128)(2,1)} %c_ref.7, ...), custom_call_target="tpu_custom_call" | custom-call | flops 10066329600 | bytes 9175040 | tf_op jit(solution)/shard_map/scan/pallas_call | solution.py:430
  96.3 0.0 copy-done.3
  96.3 0.0 collective-permute-done.3.refs_3_
  96.3 0.0 copy-start.4
  96.3 0.0 collective-permute-done.refs_0_
  96.3 0.0 copy-start.1
  96.3 0.0 collective-permute-done.1.refs_1_
  96.3 0.0 copy-start.2
  96.4 0.5 copy-done.4
  96.9 0.3 copy-done.1
  97.2 0.2 copy-done.2
  97.4 2.9 %finish.2.own_ref = bf16[768,1280]{1,0:T(8,128)(2,1)} custom-call(s32[1]{0:T(128)} %bitcast.d_ref, bf16[768,1280]{1,0:T(8,128)(2,1)} %get-tuple-element.19.own_ref, f32[3,8,256]{2,1,0:T(8,128)} %get-tuple-element.20.square_ref, bf16[256,1280]{1,0:T(8,128)(2,1)} %copy-done.1, bf16[256,1280]{1,0:T(8,128)(2,1)} %copy-done.2, ...), custom_call_target="tpu_custom_call", output_to_operand_aliasing={{}: (1, {})} | custom-call | flops 2621440 | bytes 3932160 | tf_op jit(solution)/shard_map/finish/pallas_call | solution.py:478
  100.3 0.0 collective-permute-done.5.refs_1_
  100.3 0.0 copy-start.5
  100.3 0.0 collective-permute-done.4.refs_0_
  100.3 0.6 copy-done.5
  100.9 0.0 copy-start
  100.9 0.8 copy-done
  101.7 2.4 %finish.3 = bf16[768,1280]{1,0:T(8,128)(2,1)} custom-call(s32[1]{0:T(128)} %bitcast.d_ref, bf16[768,1280]{1,0:T(8,128)(2,1)} %finish.2.own_ref, f32[3,8,256]{2,1,0:T(8,128)} %get-tuple-element.20.square_ref, bf16[256,1280]{1,0:T(8,128)(2,1)} %copy-done, f32[1,8,256]{2,1,0:T(8,128)} %copy-done.5), custom_call_target="tpu_custom_call", output_to_operand_aliasing={{}: (1, {})} | custom-call | flops 1310720 | bytes 1966080 | tf_op jit(solution)/shard_map/finish/pallas_call | solution.py:478
Async XLA Ops:
  45.3 51.1 %collective-permute-start = (bf16[256,1280]{1,0:T(8,128)(2,1)}, bf16[256,1280]{1,0:T(8,128)(2,1)S(1)}, u32[]{:S(2)}, u32[]{:S(2)}) collective-permute-start(bf16[256,1280]{1,0:T(8,128)(2,1)} %get-tuple-element.21), channel_id=1, source_target_pairs={{0,1},{1,0},{2,3},{3,2},{4,5},{5,4},{6,7},{7,6},{8,9},{9,8},{10,11... | collective-permute-start | bytes 1966088 | tf_op jit(solution)/shard_map/ppermute | solution.py:508
  46.5 9.2 %copy-start.6 = (f32[1,8,256]{2,1,0:T(8,128)S(1)}, f32[1,8,256]{2,1,0:T(8,128)}, u32[]{:S(2)}) copy-start(f32[1,8,256]{2,1,0:T(8,128)} %get-tuple-element.24) | copy-start | bytes 24580
  55.2 41.1 %collective-permute-start.1 = (bf16[256,1280]{1,0:T(8,128)(2,1)}, bf16[256,1280]{1,0:T(8,128)(2,1)S(1)}, u32[]{:S(2)}, u32[]{:S(2)}) collective-permute-start(bf16[256,1280]{1,0:T(8,128)(2,1)} %get-tuple-element.23), channel_id=1, source_target_pairs={{0,1},{1,0},{2,3},{3,2},{4,5},{5,4},{6,7},{7,6},{8,9},{9,8},{10,11... | collective-permute-start | bytes 1966088 | tf_op jit(solution)/shard_map/ppermute | solution.py:508
  55.7 21.6 %collective-permute-start.2 = (f32[1,8,256]{2,1,0:T(8,128)S(1)}, f32[1,8,256]{2,1,0:T(8,128)S(1)}, u32[]{:S(2)}, u32[]{:S(2)}) collective-permute-start(f32[1,8,256]{2,1,0:T(8,128)S(1)} %copy-done.6), channel_id=1, source_target_pairs={{0,1},{1,0},{2,3},{3,2},{4,5},{5,4},{6,7},{7,6},{8,9},{9,8},{10,11... | collective-permute-start | bytes 24584 | tf_op jit(solution)/shard_map/ppermute | solution.py:508
  57.3 39.0 %collective-permute-start.3 = (f32[1,8,256]{2,1,0:T(8,128)}, f32[1,8,256]{2,1,0:T(8,128)S(1)}, u32[]{:S(2)}, u32[]{:S(2)}) collective-permute-start(f32[1,8,256]{2,1,0:T(8,128)} %get-tuple-element.25), channel_id=1, source_target_pairs={{0,1},{1,0},{2,3},{3,2},{4,5},{5,4},{6,7},{7,6},{8,9},{9,8},{10,11... | collective-permute-start | bytes 24584 | tf_op jit(solution)/shard_map/ppermute | solution.py:508
  66.3 34.0 %collective-permute-start.4 = (bf16[256,1280]{1,0:T(8,128)(2,1)}, bf16[256,1280]{1,0:T(8,128)(2,1)S(1)}, u32[]{:S(2)}, u32[]{:S(2)}) collective-permute-start(bf16[256,1280]{1,0:T(8,128)(2,1)} %get-tuple-element.27), channel_id=1, source_target_pairs={{0,1},{1,0},{2,3},{3,2},{4,5},{5,4},{6,7},{7,6},{8,9},{9,8},{10,11... | collective-permute-start | bytes 1966088 | tf_op jit(solution)/shard_map/ppermute | solution.py:508
  77.3 19.0 %copy-start.3 = (f32[1,8,256]{2,1,0:T(8,128)}, f32[1,8,256]{2,1,0:T(8,128)S(1)}, u32[]{:S(2)}) copy-start(f32[1,8,256]{2,1,0:T(8,128)S(1)} %collective-permute-done.2.refs_2_) | copy-start | bytes 24580
  77.3 23.0 %collective-permute-start.5 = (f32[1,8,256]{2,1,0:T(8,128)}, f32[1,8,256]{2,1,0:T(8,128)S(1)}, u32[]{:S(2)}, u32[]{:S(2)}) collective-permute-start(f32[1,8,256]{2,1,0:T(8,128)} %get-tuple-element.28), channel_id=1, source_target_pairs={{0,1},{1,0},{2,3},{3,2},{4,5},{5,4},{6,7},{7,6},{8,9},{9,8},{10,11... | collective-permute-start | bytes 24584 | tf_op jit(solution)/shard_map/ppermute | solution.py:508
  96.3 0.6 copy-start.4
  96.3 0.9 copy-start.1
  96.3 1.1 %copy-start.2 = (bf16[256,1280]{1,0:T(8,128)(2,1)}, bf16[256,1280]{1,0:T(8,128)(2,1)S(1)}, u32[]{:S(2)}) copy-start(bf16[256,1280]{1,0:T(8,128)(2,1)S(1)} %collective-permute-done.1.refs_1_) | copy-start | bytes 1966084
  100.3 0.6 copy-start.5
  100.9 0.8 copy-start
